TPU v7x, 256 devices: a whole 4x4x8 slice. The times are simulated.
256 devices in a mesh: ax: 64 (over z, x, core), rad: 4 (over y).
Axes of the slice: x: 4, y: 4, z: 8, core: 2. Of those that a mesh axis runs over, the one named last changes fastest.
Arguments:
- labels: int32 [8192, 512], P('ax', 'rad'), may hold values from 0 to 2, as said below
- jitter: float32 [8192, 512], P('ax', 'rad'), may hold values from 0.8 to 1.6
Outputs:
- window_state: float32 [6, 8192, 512], P(None, 'ax', 'rad')
- time_steps: float32 [3], replicated
Inputs may be any that keep to these rules, and one draw needn't show every extreme that they name: `labels`: 0 unshocked liquid, 1 shocked liquid, 2 gas bubble.
All inputs are finite; a program needn't handle non-finite values.
Results may differ from a plain program's by a relative error of at most 0.0003.
Values sent between devices are 32-bit elements; how exact they have to be, the bound alone decides.
A program may use at most 64 MiB of HBM per device.

v0:
```python
import functools

import jax
import jax.numpy as jnp
from jax import lax
from jax.sharding import Mesh
from jax.sharding import PartitionSpec as P

WIN = 128
STEPS = 3
AX = ("ax_0", "ax_1", "ax_2")
AX_RAD = ("ax_0", "ax_1", "ax_2", "rad")


G_LIQUID = 4.4
PI_LIQUID = 1.0
G_GAS = 1.4
PI_GAS = 0.0
CFL_NUMBER = 0.3
WENO_EPS = 1e-06
ALPHA_TABLE = (0.99, 0.99, 0.01)
LIQUID_TABLE = (1.0, 1.25, 1.0)
GAS_TABLE = (0.1, 0.1, 0.1)
VELOCITY_TABLE = (0.0, 0.4, 0.0)
PRESSURE_TABLE = (1.0, 3.0, 1.0)
FLIP = (1.0, 1.0, 1.0, -1.0, 1.0, 1.0)


def one_axis_at_a_time(array, axes):
    return functools.reduce(lax.pmax, axes, array)


def extended(array, sides, width):
    for axis, dim in sides:
        peers, length = (lax.axis_size(axis), array.shape[dim])
        up = [(i, (i + 1) % peers) for i in range(peers - 1)]
        down = [(j, i) for i, j in up]
        last = lax.slice_in_dim(array, length - width, length, axis=dim)
        initial = lax.slice_in_dim(array, 0, width, axis=dim)
        before = lax.ppermute(last, axis, up)
        after = lax.ppermute(initial, axis, down)
        array = jnp.concatenate([before, array, after], axis=dim)
    return array


def passed_along(array, axis, by):
    peers = lax.axis_size(axis)
    pairs = [(i, i + by) for i in range(peers) if 0 <= i + by < peers]
    return lax.ppermute(array, axis, pairs)


def mixture(fraction):
    gamma_sum = fraction / (G_LIQUID - 1.0) + (1.0 - fraction) / (G_GAS - 1.0)
    stiff_sum = fraction * (G_LIQUID * PI_LIQUID / (G_LIQUID - 1.0)) + (1.0 - fraction) * (
        G_GAS * PI_GAS / (G_GAS - 1.0)
    )
    return (gamma_sum, stiff_sum)


def initial_fields(labels, jitter):
    phase_ids = jnp.arange(3, dtype=jnp.int32)
    onehot = (labels[None] == phase_ids[:, None, None]).astype(jnp.float32)

    def lookup(table_values):
        return jnp.sum(jnp.array(table_values, jnp.float32)[:, None, None] * onehot, axis=0)

    fraction = lookup(ALPHA_TABLE)
    part_one = fraction * lookup(LIQUID_TABLE) * jitter
    part_two = (1.0 - fraction) * lookup(GAS_TABLE) * jitter
    density = part_one + part_two
    velocity = lookup(VELOCITY_TABLE)
    pressure = lookup(PRESSURE_TABLE) * jitter
    gamma_sum, stiff_sum = mixture(fraction)
    energy = gamma_sum * pressure + stiff_sum + 0.5 * density * velocity * velocity
    return jnp.stack(
        [part_one, part_two, density * velocity, jnp.zeros_like(density), energy, fraction]
    )


def primitives(fields):
    density = fields[0] + fields[1]
    axial_speed = fields[2] / density
    radial_speed = fields[3] / density
    gamma_sum, stiff_sum = mixture(fields[5])
    pressure = (
        fields[4]
        - 0.5 * density * (axial_speed * axial_speed + radial_speed * radial_speed)
        - stiff_sum
    ) / gamma_sum
    return jnp.stack([fields[0], fields[1], axial_speed, radial_speed, pressure, fields[5]])


def speed_bound(fields):
    primitive = primitives(fields)
    density = primitive[0] + primitive[1]
    gamma_sum, stiff_sum = mixture(primitive[5])
    celerity = jnp.sqrt(((gamma_sum + 1.0) * primitive[4] + stiff_sum) / (gamma_sum * density))
    return jnp.abs(primitive[2]) + jnp.abs(primitive[3]) + celerity


def weno_side(minus_two, minus_one, middle, plus_one, plus_two):
    cand_zero = (2.0 * minus_two - 7.0 * minus_one + 11.0 * middle) / 6.0
    cand_one = (-minus_one + 5.0 * middle + 2.0 * plus_one) / 6.0
    cand_two = (2.0 * middle + 5.0 * plus_one - plus_two) / 6.0
    smooth_zero = (
        13.0 / 12.0 * (minus_two - 2.0 * minus_one + middle) ** 2
        + 0.25 * (minus_two - 4.0 * minus_one + 3.0 * middle) ** 2
    )
    smooth_one = (
        13.0 / 12.0 * (minus_one - 2.0 * middle + plus_one) ** 2
        + 0.25 * (minus_one - plus_one) ** 2
    )
    smooth_two = (
        13.0 / 12.0 * (middle - 2.0 * plus_one + plus_two) ** 2
        + 0.25 * (3.0 * middle - 4.0 * plus_one + plus_two) ** 2
    )
    weight_zero = 0.1 / (WENO_EPS + smooth_zero) ** 2
    weight_one = 0.6 / (WENO_EPS + smooth_one) ** 2
    weight_two = 0.3 / (WENO_EPS + smooth_two) ** 2
    return (weight_zero * cand_zero + weight_one * cand_one + weight_two * cand_two) / (
        weight_zero + weight_one + weight_two
    )


def interfaces(primitive, along_axis):
    span_count = primitive.shape[along_axis] - 5
    stencil = [
        lax.slice_in_dim(primitive, offset, offset + span_count, axis=along_axis)
        for offset in range(6)
    ]
    left_state = weno_side(stencil[0], stencil[1], stencil[2], stencil[3], stencil[4])
    right_state = weno_side(stencil[5], stencil[4], stencil[3], stencil[2], stencil[1])
    return (left_state, right_state)


def hllc_flux(left_state, right_state, normal):
    tangent = 5 - normal

    def side_terms(primitive):
        density = primitive[0] + primitive[1]
        gamma_sum, stiff_sum = mixture(primitive[5])
        normal_speed = primitive[normal]
        tangent_speed = primitive[tangent]
        pressure = primitive[4]
        energy = (
            gamma_sum * pressure
            + stiff_sum
            + 0.5 * density * (normal_speed * normal_speed + tangent_speed * tangent_speed)
        )
        celerity = jnp.sqrt(((gamma_sum + 1.0) * pressure + stiff_sum) / (gamma_sum * density))
        return (density, normal_speed, tangent_speed, pressure, energy, celerity)

    left_values = side_terms(left_state)
    right_values = side_terms(right_state)
    speed_low = jnp.minimum(left_values[1] - left_values[5], right_values[1] - right_values[5])
    speed_high = jnp.maximum(left_values[1] + left_values[5], right_values[1] + right_values[5])
    left_mass = left_values[0] * (speed_low - left_values[1])
    right_mass = right_values[0] * (speed_high - right_values[1])
    star_speed = (
        right_values[3] - left_values[3] + left_mass * left_values[1] - right_mass * right_values[1]
    ) / (left_mass - right_mass)

    def arrange(first_part, second_part, normal_part, tangent_part, energy_part):
        components = [first_part, second_part, None, None, energy_part]
        components[normal] = normal_part
        components[tangent] = tangent_part
        return components

    def physical(primitive, side_values):
        density, normal_speed, tangent_speed, pressure, energy, celerity = side_values
        return arrange(
            primitive[0] * normal_speed,
            primitive[1] * normal_speed,
            density * normal_speed * normal_speed + pressure,
            density * normal_speed * tangent_speed,
            (energy + pressure) * normal_speed,
        )

    def conserved(primitive, side_values):
        density, normal_speed, tangent_speed, pressure, energy, celerity = side_values
        return arrange(
            primitive[0], primitive[1], density * normal_speed, density * tangent_speed, energy
        )

    def starred(primitive, side_values, wave_speed):
        density, normal_speed, tangent_speed, pressure, energy, celerity = side_values
        factor = (wave_speed - normal_speed) / (wave_speed - star_speed)
        star_energy = energy + (star_speed - normal_speed) * (
            density * star_speed + pressure / (wave_speed - normal_speed)
        )
        return arrange(
            factor * primitive[0],
            factor * primitive[1],
            factor * density * star_speed,
            factor * density * tangent_speed,
            factor * star_energy,
        )

    left_flux = physical(left_state, left_values)
    right_flux = physical(right_state, right_values)
    left_cons = conserved(left_state, left_values)
    right_cons = conserved(right_state, right_values)
    left_star = starred(left_state, left_values, speed_low)
    right_star = starred(right_state, right_values, speed_high)
    fluxes = []
    for component in range(5):
        left_star_flux = left_flux[component] + speed_low * (
            left_star[component] - left_cons[component]
        )
        right_star_flux = right_flux[component] + speed_high * (
            right_star[component] - right_cons[component]
        )
        fluxes.append(
            jnp.where(
                speed_low >= 0.0,
                left_flux[component],
                jnp.where(
                    star_speed >= 0.0,
                    left_star_flux,
                    jnp.where(speed_high >= 0.0, right_star_flux, right_flux[component]),
                ),
            )
        )
    fluxes.append(star_speed * jnp.where(star_speed >= 0.0, left_state[5], right_state[5]))
    return (jnp.stack(fluxes), star_speed)


def section_rhs(padded, radius):
    primitive = primitives(padded)
    axial_flux, axial_star = hllc_flux(*interfaces(primitive[:, :, 3:-3], 1), 2)
    radial_flux, radial_star = hllc_flux(*interfaces(primitive[:, 3:-3, :], 2), 3)
    centre = primitive[:, 3:-3, 3:-3]
    energy = padded[4, 3:-3, 3:-3]
    divergence = (
        axial_flux[:, 1:] - axial_flux[:, :-1] + (radial_flux[:, :, 1:] - radial_flux[:, :, :-1])
    )
    stretch = axial_star[1:] - axial_star[:-1] + (radial_star[:, 1:] - radial_star[:, :-1])
    density = centre[0] + centre[1]
    radial_speed = centre[3]
    inverse = radial_speed / radius
    source = [
        centre[0] * inverse,
        centre[1] * inverse,
        density * centre[2] * inverse,
        density * radial_speed * inverse,
        (energy + centre[4]) * inverse,
    ]
    rates = [-divergence[component] - source[component] for component in range(5)]
    rates.append(-divergence[5] + centre[5] * stretch)
    return jnp.stack(rates)


def fill_edges(padded, margin, axial_first, axial_last, radial_first, radial_last):
    flip_sign = jnp.array(FLIP, jnp.float32)[:, None, None]
    mirror = padded[:, :, margin : 2 * margin][:, :, ::-1] * flip_sign
    padded = jnp.where(
        radial_first, jnp.concatenate([mirror, padded[:, :, margin:]], axis=2), padded
    )
    top_row = padded[:, :, -margin - 1 : -margin]
    padded = jnp.where(
        radial_last,
        jnp.concatenate([padded[:, :, :-margin], jnp.repeat(top_row, margin, axis=2)], axis=2),
        padded,
    )
    low_column = padded[:, margin : margin + 1, :]
    padded = jnp.where(
        axial_first,
        jnp.concatenate([jnp.repeat(low_column, margin, axis=1), padded[:, margin:, :]], axis=1),
        padded,
    )
    high_column = padded[:, -margin - 1 : -margin, :]
    padded = jnp.where(
        axial_last,
        jnp.concatenate([padded[:, :-margin, :], jnp.repeat(high_column, margin, axis=1)], axis=1),
        padded,
    )
    return padded


def shards(labels, jitter):
    block_x, block_r = labels.shape
    axial_index = lax.axis_index(AX)
    radial_index = lax.axis_index("rad")
    axial_count = lax.axis_size(AX)
    radial_count = lax.axis_size("rad")
    axial_first = axial_index == 0
    axial_last = axial_index == axial_count - 1
    radial_first = radial_index == 0
    radial_last = radial_index == radial_count - 1
    row_offset = (radial_index * block_r).astype(jnp.float32)

    def radius_for(margin):
        return row_offset + jnp.arange(-margin, block_r + margin, dtype=jnp.float32) + 0.5

    def edged(padded, margin):
        return fill_edges(padded, margin, axial_first, axial_last, radial_first, radial_last)

    fields = initial_fields(labels, jitter)
    step_sizes = []
    for step_index in range(STEPS):
        time_step = CFL_NUMBER / one_axis_at_a_time(jnp.max(speed_bound(fields)), AX_RAD)
        padded = extended(fields, ((AX, 1), ("rad", 2)), 9)
        padded = edged(padded, 9)
        first_section = padded[:, 3:-3, 3:-3] + time_step * section_rhs(padded, radius_for(6))
        first_section = edged(first_section, 6)
        second_section = 0.75 * padded[:, 6:-6, 6:-6] + 0.25 * (
            first_section[:, 3:-3, 3:-3] + time_step * section_rhs(first_section, radius_for(3))
        )
        second_section = edged(second_section, 3)
        fields = 1.0 / 3.0 * padded[:, 9:-9, 9:-9] + 2.0 / 3.0 * (
            second_section[:, 3:-3, 3:-3] + time_step * section_rhs(second_section, radius_for(0))
        )
        step_sizes.append(time_step)
    quotient = WIN // block_x
    near_part = passed_along(fields, AX, -quotient)
    shifted = near_part
    column_ids = axial_index * block_x + jnp.arange(block_x, dtype=jnp.int32) + WIN
    beyond = column_ids >= axial_count * block_x
    ambient = initial_fields(jnp.zeros((1, 1), jnp.int32), jnp.ones((1, 1), jnp.float32))
    shifted = jnp.where(beyond[None, :, None], ambient, shifted)
    return (shifted, jnp.stack(step_sizes))


def solution(mesh):
    torus = Mesh(mesh.devices.reshape(8, 4, 2, mesh.shape["rad"]), ("ax_0", "ax_1", "ax_2", "rad"))
    in_specs = (P(AX, "rad"), P(AX, "rad"))
    out_specs = (P(None, AX, "rad"), P())
    return jax.shard_map(
        shards, mesh=torus, in_specs=in_specs, out_specs=out_specs, check_vma=False
    )
```

profile of v0, /device:TPU:41, one launch (start us, length us, event | category | flops | bytes accessed | tf_op | source)
XLA Modules:
  0.0 335.2 jit_solution(4012297045934632597)
XLA Ops:
  0.7 0.6 copy-done.6
  1.3 1.0 select_reduce_fusion
  2.5 0.7 copy-done
  4.0 3.7 %collective-permute-start = (f32[6,9,128]{1,2,0:T(8,128)S(1)}, f32[6,9,128]{1,2,0:T(8,128)S(1)}, u32[]{:S(2)}, u32[]{:S(2)}) collective-permute-start(f32[6,9,128]{1,2,0:T(8,128)S(1)} %get-tuple-element.257), channel_id=1, source_target_pairs={{0,4},{4,8},{8,12},{12,16},{16,20},{20,24},{24,28},{28,32},{32,36}... | collective-permute-start | bytes 82952 | tf_op jit(solution)/shard_map/ppermute | solution.py:40
  7.7 1.9 collective-permute-start.1
  9.6 0.7 add_reduce_fusion.2
  10.4 14.7 %pmax.84 = f32[]{:T(128)} all-reduce(f32[]{:T(128)} %add_reduce_fusion.2), channel_id=1, replica_groups=mesh['ax_0'=8,'ax_1'=4,'ax_2'=2,'rad'=4] {'ax_0'}, use_global_device_ids=true, to_apply=%region_11.12 | all-reduce | flops 1 | bytes 8 | tf_op jit(solution)/shard_map/pmax | solution.py:30
  25.1 8.8 %pmax.85 = f32[]{:T(128)} all-reduce(f32[]{:T(128)} %pmax.84), channel_id=1, replica_groups=mesh['ax_0'=8,'ax_1'=4,'ax_2'=2,'rad'=4] {'ax_1'}, use_global_device_ids=true, to_apply=%region_12.13 | all-reduce | flops 1 | bytes 8 | tf_op jit(solution)/shard_map/pmax | solution.py:30
  33.9 9.5 %pmax.86 = f32[]{:T(128)} all-reduce(f32[]{:T(128)} %pmax.85), channel_id=1, replica_groups=mesh['ax_0'=8,'ax_1'=4,'ax_2'=2,'rad'=4] {'ax_2'}, use_global_device_ids=true, to_apply=%region_13.14 | all-reduce | flops 1 | bytes 8 | tf_op jit(solution)/shard_map/pmax | solution.py:30
  43.4 7.3 %pmax.87 = f32[]{:T(128)} all-reduce(f32[]{:T(128)} %pmax.86), channel_id=1, replica_groups=mesh['ax_0'=8,'ax_1'=4,'ax_2'=2,'rad'=4] {'rad'}, use_global_device_ids=true, to_apply=%region_14.15 | all-reduce | flops 1 | bytes 8 | tf_op jit(solution)/shard_map/pmax | solution.py:30
  51.6 4.1 %collective-permute-start.2 = (f32[6,146,9]{1,2,0:T(8,128)S(1)}, f32[6,146,9]{1,2,0:T(8,128)S(1)}, u32[]{:S(2)}, u32[]{:S(2)}) collective-permute-start(f32[6,146,9]{1,2,0:T(8,128)S(1)} %get-tuple-element.216), channel_id=1, source_target_pairs={{1,0},{2,1},{3,2},{5,4},{6,5},{7,6},{9,8},{10,9},{11,10},{13,12},{... | collective-permute-start | bytes 94616 | tf_op jit(solution)/shard_map/ppermute | solution.py:41
  55.8 1.9 collective-permute-start.3
  57.8 3.3 collective-permute-done.3
  64.2 4.5 %fusion.127 = (f32[6,141,140]{1,2,0:T(8,128)S(1)}, f32[6,141,140]{1,2,0:T(8,128)S(1)}) fusion(f32[6,146,146]{1,2,0:T(8,128)S(1)} %constant_dynamic-update-slice_fusion.6), kind=kLoop, calls=%fused_computation.194 | loop fusion | flops 14686560 | bytes 3790080 | tf_op jit(solution)/shard_map/div | solution.py:120
  68.7 4.5 %fusion.105 = (f32[6,140,141]{1,2,0:T(8,128)S(1)}, f32[6,140,141]{1,2,0:T(8,128)S(1)}) fusion(f32[6,146,146]{1,2,0:T(8,128)S(1)} %constant_dynamic-update-slice_fusion.6), kind=kLoop, calls=%fused_computation.167 | loop fusion | flops 14686560 | bytes 3790080 | tf_op jit(solution)/shard_map/div | solution.py:120
  81.2 4.1 %fusion.268 = (f32[6,135,134]{1,2,0:T(8,128)S(1)}, f32[6,135,134]{1,2,0:T(8,128)S(1)}) fusion(f32[6,140,140]{1,2,0:T(8,128)S(1)} %constant_dynamic-update-slice_fusion.29), kind=kLoop, calls=%fused_computation.389 | loop fusion | flops 13458960 | bytes 3473280 | tf_op jit(solution)/shard_map/div | solution.py:120
  85.3 4.5 %fusion.246 = (f32[6,134,135]{1,2,0:T(8,128)S(1)}, f32[6,134,135]{1,2,0:T(8,128)S(1)}) fusion(f32[6,140,140]{1,2,0:T(8,128)S(1)} %constant_dynamic-update-slice_fusion.29), kind=kLoop, calls=%fused_computation.362 | loop fusion | flops 13458960 | bytes 3473280 | tf_op jit(solution)/shard_map/div | solution.py:120
  94.4 0.5 fusion.146
  97.8 4.3 %fusion.334 = (f32[6,129,128]{1,2,0:T(8,128)S(1)}, f32[6,129,128]{1,2,0:T(8,128)S(1)}) fusion(f32[6,134,134]{1,2,0:T(8,128)S(1)} %constant_dynamic-update-slice_fusion.52), kind=kLoop, calls=%fused_computation.470 | loop fusion | flops 12284928 | bytes 3170304 | tf_op jit(solution)/shard_map/div | solution.py:120
  102.0 2.3 fusion.400
  108.2 6.7 %collective-permute-start.4 = (f32[6,9,128]{1,2,0:T(8,128)S(1)}, f32[6,9,128]{1,2,0:T(8,128)S(1)}, u32[]{:S(2)}, u32[]{:S(2)}) collective-permute-start(f32[6,9,128]{1,2,0:T(8,128)S(1)} %get-tuple-element.255), channel_id=1, source_target_pairs={{0,4},{4,8},{8,12},{12,16},{16,20},{20,24},{24,28},{28,32},{32,36}... | collective-permute-start | bytes 82952 | tf_op jit(solution)/shard_map/ppermute | solution.py:40
  114.9 1.9 collective-permute-start.5
  116.8 0.7 add_reduce_fusion.1
  117.5 13.3 %pmax.88 = f32[]{:T(128)} all-reduce(f32[]{:T(128)} %add_reduce_fusion.1), channel_id=1, replica_groups=mesh['ax_0'=8,'ax_1'=4,'ax_2'=2,'rad'=4] {'ax_0'}, use_global_device_ids=true, to_apply=%region_16.17 | all-reduce | flops 1 | bytes 8 | tf_op jit(solution)/shard_map/pmax | solution.py:30
  130.7 8.1 %pmax.89 = f32[]{:T(128)} all-reduce(f32[]{:T(128)} %pmax.88), channel_id=1, replica_groups=mesh['ax_0'=8,'ax_1'=4,'ax_2'=2,'rad'=4] {'ax_1'}, use_global_device_ids=true, to_apply=%region_17.18 | all-reduce | flops 1 | bytes 8 | tf_op jit(solution)/shard_map/pmax | solution.py:30
  138.9 10.0 %pmax.90 = f32[]{:T(128)} all-reduce(f32[]{:T(128)} %pmax.89), channel_id=1, replica_groups=mesh['ax_0'=8,'ax_1'=4,'ax_2'=2,'rad'=4] {'ax_2'}, use_global_device_ids=true, to_apply=%region_18.19 | all-reduce | flops 1 | bytes 8 | tf_op jit(solution)/shard_map/pmax | solution.py:30
  148.9 5.9 %pmax.91 = f32[]{:T(128)} all-reduce(f32[]{:T(128)} %pmax.90), channel_id=1, replica_groups=mesh['ax_0'=8,'ax_1'=4,'ax_2'=2,'rad'=4] {'rad'}, use_global_device_ids=true, to_apply=%region_19.20 | all-reduce | flops 1 | bytes 8 | tf_op jit(solution)/shard_map/pmax | solution.py:30
  155.8 4.0 %collective-permute-start.6 = (f32[6,146,9]{1,2,0:T(8,128)S(1)}, f32[6,146,9]{1,2,0:T(8,128)S(1)}, u32[]{:S(2)}, u32[]{:S(2)}) collective-permute-start(f32[6,146,9]{1,2,0:T(8,128)S(1)} %get-tuple-element.214), channel_id=1, source_target_pairs={{1,0},{2,1},{3,2},{5,4},{6,5},{7,6},{9,8},{10,9},{11,10},{13,12},{... | collective-permute-start | bytes 94616 | tf_op jit(solution)/shard_map/ppermute | solution.py:41
  159.9 1.9 collective-permute-start.7
  161.9 3.3 collective-permute-done.7
  168.2 4.5 %fusion.83 = (f32[6,141,140]{1,2,0:T(8,128)S(1)}, f32[6,141,140]{1,2,0:T(8,128)S(1)}) fusion(f32[6,146,146]{1,2,0:T(8,128)S(1)} %constant_dynamic-update-slice_fusion.75), kind=kLoop, calls=%fused_computation.140 | loop fusion | flops 14686560 | bytes 3790080 | tf_op jit(solution)/shard_map/div | solution.py:120
  172.7 4.5 %fusion.61 = (f32[6,140,141]{1,2,0:T(8,128)S(1)}, f32[6,140,141]{1,2,0:T(8,128)S(1)}) fusion(f32[6,146,146]{1,2,0:T(8,128)S(1)} %constant_dynamic-update-slice_fusion.75), kind=kLoop, calls=%fused_computation.113 | loop fusion | flops 14686560 | bytes 3790080 | tf_op jit(solution)/shard_map/div | solution.py:120
  185.3 4.1 %fusion.224 = (f32[6,135,134]{1,2,0:T(8,128)S(1)}, f32[6,135,134]{1,2,0:T(8,128)S(1)}) fusion(f32[6,140,140]{1,2,0:T(8,128)S(1)} %constant_dynamic-update-slice_fusion.98), kind=kLoop, calls=%fused_computation.335 | loop fusion | flops 13458960 | bytes 3473280 | tf_op jit(solution)/shard_map/div | solution.py:120
  189.4 4.5 %fusion.202 = (f32[6,134,135]{1,2,0:T(8,128)S(1)}, f32[6,134,135]{1,2,0:T(8,128)S(1)}) fusion(f32[6,140,140]{1,2,0:T(8,128)S(1)} %constant_dynamic-update-slice_fusion.98), kind=kLoop, calls=%fused_computation.308 | loop fusion | flops 13458960 | bytes 3473280 | tf_op jit(solution)/shard_map/div | solution.py:120
  198.5 0.5 fusion.143
  201.8 4.3 %fusion.312 = (f32[6,129,128]{1,2,0:T(8,128)S(1)}, f32[6,129,128]{1,2,0:T(8,128)S(1)}) fusion(f32[6,134,134]{1,2,0:T(8,128)S(1)} %constant_dynamic-update-slice_fusion.121), kind=kLoop, calls=%fused_computation.443 | loop fusion | flops 12284928 | bytes 3170304 | tf_op jit(solution)/shard_map/div | solution.py:120
  206.1 2.3 fusion.378
  212.1 0.7 add_reduce_fusion
  212.8 13.2 %pmax.92 = f32[]{:T(128)} all-reduce(f32[]{:T(128)} %add_reduce_fusion), channel_id=1, replica_groups=mesh['ax_0'=8,'ax_1'=4,'ax_2'=2,'rad'=4] {'ax_0'}, use_global_device_ids=true, to_apply=%region_21.22 | all-reduce | flops 1 | bytes 8 | tf_op jit(solution)/shard_map/pmax | solution.py:30
  225.9 8.3 %pmax.93 = f32[]{:T(128)} all-reduce(f32[]{:T(128)} %pmax.92), channel_id=1, replica_groups=mesh['ax_0'=8,'ax_1'=4,'ax_2'=2,'rad'=4] {'ax_1'}, use_global_device_ids=true, to_apply=%region_22.23 | all-reduce | flops 1 | bytes 8 | tf_op jit(solution)/shard_map/pmax | solution.py:30
  234.5 12.3 %pmax.94 = f32[]{:T(128)} all-reduce(f32[]{:T(128)} %pmax.93), channel_id=1, replica_groups=mesh['ax_0'=8,'ax_1'=4,'ax_2'=2,'rad'=4] {'ax_2'}, use_global_device_ids=true, to_apply=%region_23.24 | all-reduce | flops 1 | bytes 8 | tf_op jit(solution)/shard_map/pmax | solution.py:30
  246.8 1.9 collective-permute-start.8
  248.7 2.4 collective-permute-start.9
  251.1 0.6 select_reduce_fusion.8
  251.7 6.5 %pmax.95 = f32[]{:T(128)} all-reduce(f32[]{:T(128)} %pmax.94), channel_id=1, replica_groups=mesh['ax_0'=8,'ax_1'=4,'ax_2'=2,'rad'=4] {'rad'}, use_global_device_ids=true, to_apply=%region_24.25 | all-reduce | flops 1 | bytes 8 | tf_op jit(solution)/shard_map/pmax | solution.py:30
  259.2 3.7 %collective-permute-start.10 = (f32[6,146,9]{1,2,0:T(8,128)S(1)}, f32[6,146,9]{1,2,0:T(8,128)S(1)}, u32[]{:S(2)}, u32[]{:S(2)}) collective-permute-start(f32[6,146,9]{1,2,0:T(8,128)S(1)} %get-tuple-element.212), channel_id=1, source_target_pairs={{1,0},{2,1},{3,2},{5,4},{6,5},{7,6},{9,8},{10,9},{11,10},{13,12},{... | collective-permute-start | bytes 94616 | tf_op jit(solution)/shard_map/ppermute | solution.py:41
  263.0 1.9 collective-permute-start.11
  265.0 3.3 collective-permute-done.11
  269.3 0.5 slice_reduce_fusion.1
  271.4 4.5 %fusion.39 = (f32[6,141,140]{1,2,0:T(8,128)S(1)}, f32[6,141,140]{1,2,0:T(8,128)S(1)}) fusion(f32[6,146,146]{1,2,0:T(8,128)S(1)} %constant_dynamic-update-slice_fusion.144), kind=kLoop, calls=%fused_computation.86 | loop fusion | flops 14686560 | bytes 3790080 | tf_op jit(solution)/shard_map/div | solution.py:120
  275.9 4.5 %fusion.17 = (f32[6,140,141]{1,2,0:T(8,128)S(1)}, f32[6,140,141]{1,2,0:T(8,128)S(1)}) fusion(f32[6,146,146]{1,2,0:T(8,128)S(1)} %constant_dynamic-update-slice_fusion.144), kind=kLoop, calls=%fused_computation.59 | loop fusion | flops 14686560 | bytes 3790080 | tf_op jit(solution)/shard_map/div | solution.py:120
  288.4 4.1 %fusion.180 = (f32[6,135,134]{1,2,0:T(8,128)S(1)}, f32[6,135,134]{1,2,0:T(8,128)S(1)}) fusion(f32[6,140,140]{1,2,0:T(8,128)S(1)} %constant_dynamic-update-slice_fusion.167), kind=kLoop, calls=%fused_computation.281 | loop fusion | flops 13458960 | bytes 3473280 | tf_op jit(solution)/shard_map/div | solution.py:120
  292.5 4.5 %fusion.158 = (f32[6,134,135]{1,2,0:T(8,128)S(1)}, f32[6,134,135]{1,2,0:T(8,128)S(1)}) fusion(f32[6,140,140]{1,2,0:T(8,128)S(1)} %constant_dynamic-update-slice_fusion.167), kind=kLoop, calls=%fused_computation.254 | loop fusion | flops 13458960 | bytes 3473280 | tf_op jit(solution)/shard_map/div | solution.py:120
  301.6 0.5 fusion.140
  305.0 4.1 %fusion.290 = (f32[6,129,128]{1,2,0:T(8,128)S(1)}, f32[6,129,128]{1,2,0:T(8,128)S(1)}) fusion(f32[6,134,134]{1,2,0:T(8,128)S(1)} %constant_dynamic-update-slice_fusion.190), kind=kLoop, calls=%fused_computation.416 | loop fusion | flops 12284928 | bytes 3170304 | tf_op jit(solution)/shard_map/div | solution.py:120
  309.1 2.3 fusion.356
  315.1 8.8 %collective-permute-start.12 = (f32[6,128,128]{1,2,0:T(8,128)S(1)}, f32[6,128,128]{1,2,0:T(8,128)S(1)}, u32[]{:S(2)}, u32[]{:S(2)}) collective-permute-start(f32[6,128,128]{1,2,0:T(8,128)S(1)} %fusion.413), channel_id=1, source_target_pairs={{4,0},{8,4},{12,8},{16,12},{20,16},{24,20},{28,24},{32,28},{36,32}... | collective-permute-start | bytes 1179656 | tf_op jit(solution)/shard_map/ppermute | solution.py:49
  323.8 0.6 select_reduce_fusion.6
  326.4 0.6 select_reduce_fusion.7
  330.7 0.6 copy-done.5
  331.4 0.6 select_reduce_fusion.5
  332.6 0.7 stack.136
  333.4 0.6 pad_maximum_fusion.18
  334.1 0.9 copy.92
  (429 shorter events, 66.2 us)
Async XLA Ops:
  0.6 0.7 copy-start.6
  0.6 0.7 copy-start.2
  0.7 0.7 copy-start.3
  0.7 0.7 copy-start.4
  2.4 0.8 copy-start
  4.0 47.3 %collective-permute-start = (f32[6,9,128]{1,2,0:T(8,128)S(1)}, f32[6,9,128]{1,2,0:T(8,128)S(1)}, u32[]{:S(2)}, u32[]{:S(2)}) collective-permute-start(f32[6,9,128]{1,2,0:T(8,128)S(1)} %get-tuple-element.257), channel_id=1, source_target_pairs={{0,4},{4,8},{8,12},{12,16},{16,20},{20,24},{24,28},{28,32},{32,36}... | collective-permute-start | bytes 82952 | tf_op jit(solution)/shard_map/ppermute | solution.py:40
  7.7 43.7 %collective-permute-start.1 = (f32[6,9,128]{1,2,0:T(8,128)S(1)}, f32[6,9,128]{1,2,0:T(8,128)S(1)}, u32[]{:S(2)}, u32[]{:S(2)}) collective-permute-start(f32[6,9,128]{1,2,0:T(8,128)S(1)} %get-tuple-element.258), channel_id=1, source_target_pairs={{4,0},{8,4},{12,8},{16,12},{20,16},{24,20},{28,24},{32,28},{36,32}... | collective-permute-start | bytes 82952 | tf_op jit(solution)/shard_map/ppermute | solution.py:41
  51.6 6.1 %copy-start.1 = (f32[6]{0:T(128)S(1)}, f32[6]{0:T(128)}, u32[]{:S(2)}) copy-start(f32[6]{0:T(128)} %constant.456.clone) | copy-start | bytes 76
  51.6 6.2 %collective-permute-start.2 = (f32[6,146,9]{1,2,0:T(8,128)S(1)}, f32[6,146,9]{1,2,0:T(8,128)S(1)}, u32[]{:S(2)}, u32[]{:S(2)}) collective-permute-start(f32[6,146,9]{1,2,0:T(8,128)S(1)} %get-tuple-element.216), channel_id=1, source_target_pairs={{1,0},{2,1},{3,2},{5,4},{6,5},{7,6},{9,8},{10,9},{11,10},{13,12},{... | collective-permute-start | bytes 94616 | tf_op jit(solution)/shard_map/ppermute | solution.py:41
  55.8 5.4 %collective-permute-start.3 = (f32[6,146,9]{1,2,0:T(8,128)S(1)}, f32[6,146,9]{1,2,0:T(8,128)S(1)}, u32[]{:S(2)}, u32[]{:S(2)}) collective-permute-start(f32[6,146,9]{1,2,0:T(8,128)S(1)} %get-tuple-element.215), channel_id=1, source_target_pairs={{0,1},{1,2},{2,3},{4,5},{5,6},{6,7},{8,9},{9,10},{10,11},{12,13},{... | collective-permute-start | bytes 94616 | tf_op jit(solution)/shard_map/ppermute | solution.py:40
  108.2 47.4 %collective-permute-start.4 = (f32[6,9,128]{1,2,0:T(8,128)S(1)}, f32[6,9,128]{1,2,0:T(8,128)S(1)}, u32[]{:S(2)}, u32[]{:S(2)}) collective-permute-start(f32[6,9,128]{1,2,0:T(8,128)S(1)} %get-tuple-element.255), channel_id=1, source_target_pairs={{0,4},{4,8},{8,12},{12,16},{16,20},{20,24},{24,28},{28,32},{32,36}... | collective-permute-start | bytes 82952 | tf_op jit(solution)/shard_map/ppermute | solution.py:40
  114.9 40.7 %collective-permute-start.5 = (f32[6,9,128]{1,2,0:T(8,128)S(1)}, f32[6,9,128]{1,2,0:T(8,128)S(1)}, u32[]{:S(2)}, u32[]{:S(2)}) collective-permute-start(f32[6,9,128]{1,2,0:T(8,128)S(1)} %get-tuple-element.256), channel_id=1, source_target_pairs={{4,0},{8,4},{12,8},{16,12},{20,16},{24,20},{28,24},{32,28},{36,32}... | collective-permute-start | bytes 82952 | tf_op jit(solution)/shard_map/ppermute | solution.py:41
  155.8 6.1 %collective-permute-start.6 = (f32[6,146,9]{1,2,0:T(8,128)S(1)}, f32[6,146,9]{1,2,0:T(8,128)S(1)}, u32[]{:S(2)}, u32[]{:S(2)}) collective-permute-start(f32[6,146,9]{1,2,0:T(8,128)S(1)} %get-tuple-element.214), channel_id=1, source_target_pairs={{1,0},{2,1},{3,2},{5,4},{6,5},{7,6},{9,8},{10,9},{11,10},{13,12},{... | collective-permute-start | bytes 94616 | tf_op jit(solution)/shard_map/ppermute | solution.py:41
  159.9 5.4 %collective-permute-start.7 = (f32[6,146,9]{1,2,0:T(8,128)S(1)}, f32[6,146,9]{1,2,0:T(8,128)S(1)}, u32[]{:S(2)}, u32[]{:S(2)}) collective-permute-start(f32[6,146,9]{1,2,0:T(8,128)S(1)} %get-tuple-element.213), channel_id=1, source_target_pairs={{0,1},{1,2},{2,3},{4,5},{5,6},{6,7},{8,9},{9,10},{10,11},{12,13},{... | collective-permute-start | bytes 94616 | tf_op jit(solution)/shard_map/ppermute | solution.py:40
  246.8 12.2 %collective-permute-start.8 = (f32[6,9,128]{1,2,0:T(8,128)S(1)}, f32[6,9,128]{1,2,0:T(8,128)S(1)}, u32[]{:S(2)}, u32[]{:S(2)}) collective-permute-start(f32[6,9,128]{1,2,0:T(8,128)S(1)} %get-tuple-element.253), channel_id=1, source_target_pairs={{0,4},{4,8},{8,12},{12,16},{16,20},{20,24},{24,28},{28,32},{32,36}... | collective-permute-start | bytes 82952 | tf_op jit(solution)/shard_map/ppermute | solution.py:40
  248.7 10.3 %collective-permute-start.9 = (f32[6,9,128]{1,2,0:T(8,128)S(1)}, f32[6,9,128]{1,2,0:T(8,128)S(1)}, u32[]{:S(2)}, u32[]{:S(2)}) collective-permute-start(f32[6,9,128]{1,2,0:T(8,128)S(1)} %get-tuple-element.254), channel_id=1, source_target_pairs={{4,0},{8,4},{12,8},{16,12},{20,16},{24,20},{28,24},{32,28},{36,32}... | collective-permute-start | bytes 82952 | tf_op jit(solution)/shard_map/ppermute | solution.py:41
  259.2 5.8 %collective-permute-start.10 = (f32[6,146,9]{1,2,0:T(8,128)S(1)}, f32[6,146,9]{1,2,0:T(8,128)S(1)}, u32[]{:S(2)}, u32[]{:S(2)}) collective-permute-start(f32[6,146,9]{1,2,0:T(8,128)S(1)} %get-tuple-element.212), channel_id=1, source_target_pairs={{1,0},{2,1},{3,2},{5,4},{6,5},{7,6},{9,8},{10,9},{11,10},{13,12},{... | collective-permute-start | bytes 94616 | tf_op jit(solution)/shard_map/ppermute | solution.py:41
  263.0 5.4 %collective-permute-start.11 = (f32[6,146,9]{1,2,0:T(8,128)S(1)}, f32[6,146,9]{1,2,0:T(8,128)S(1)}, u32[]{:S(2)}, u32[]{:S(2)}) collective-permute-start(f32[6,146,9]{1,2,0:T(8,128)S(1)} %get-tuple-element.211), channel_id=1, source_target_pairs={{0,1},{1,2},{2,3},{4,5},{5,6},{6,7},{8,9},{9,10},{10,11},{12,13},{... | collective-permute-start | bytes 94616 | tf_op jit(solution)/shard_map/ppermute | solution.py:40
  314.8 9.1 %copy-start.7 = (f32[3]{0:T(128)S(1)}, f32[3]{0:T(128)}, u32[]{:S(2)}) copy-start(f32[3]{0:T(128)} %constant.454.clone) | copy-start | bytes 40
  315.1 18.9 %collective-permute-start.12 = (f32[6,128,128]{1,2,0:T(8,128)S(1)}, f32[6,128,128]{1,2,0:T(8,128)S(1)}, u32[]{:S(2)}, u32[]{:S(2)}) collective-permute-start(f32[6,128,128]{1,2,0:T(8,128)S(1)} %fusion.413), channel_id=1, source_target_pairs={{4,0},{8,4},{12,8},{16,12},{20,16},{24,20},{28,24},{32,28},{36,32}... | collective-permute-start | bytes 1179656 | tf_op jit(solution)/shard_map/ppermute | solution.py:49
  330.7 0.7 copy-start.5
where the time goes:
time: 340 us; the launch traced here: 335 us
  other arithmetic  130 us (38%)
  blocking collectives  118 us (35%)
  starting transfers between devices  44.9 us (13%)
  local copies, waits for them, and re-layouts  20.9 us (6%)
  between operations  11.8 us (3%)
  waiting for transfers between devices  10.1 us (3%)
    pmax x12, blocking collectives, one_axis_at_a_time(): return functools.reduce(lax.pmax, axes, array)  118 us
    div x18, other arithmetic, weno_side(): (weight_zero * cand_zero + weight_one * cand_one + weight_two * cand_two)...  72.4 us
    unnamed x166, other arithmetic  29.8 us
    ppermute x6, starting transfers between devices, extended(): after = lax.ppermute(initial, axis, down)  18.2 us
    ppermute x6, starting transfers between devices, extended(): before = lax.ppermute(last, axis, up)  18 us
    ppermute x6, waiting for transfers between devices, extended(): before = lax.ppermute(last, axis, up)  10 us
    ppermute x1, starting transfers between devices, passed_along(): return lax.ppermute(array, axis, pairs)  8.75 us
  transfers between devices with their start and end apart: 13, of which 3 were waited for; matrix products, arithmetic and copies ran while one was open for 2% of the time, Pallas kernels for 0%

commit v1 on v0

v1 whole, which is shorter than its diff:
```python
import functools

import jax
import jax.numpy as jnp
from jax import lax
from jax.experimental import pallas as pl
from jax.experimental.pallas import tpu as pltpu
from jax.sharding import PartitionSpec as P

MESH = pl.DeviceIdType.MESH

STEPS = 3
STAGES = 3 * STEPS
X_CHIPS = 4

G_LIQUID = 4.4
PI_LIQUID = 1.0
G_GAS = 1.4
PI_GAS = 0.0
CFL_NUMBER = 0.3
WENO_EPS = 1e-06
ALPHA_TABLE = (0.99, 0.99, 0.01)
LIQUID_TABLE = (1.0, 1.25, 1.0)
GAS_TABLE = (0.1, 0.1, 0.1)
VELOCITY_TABLE = (0.0, 0.4, 0.0)
PRESSURE_TABLE = (1.0, 3.0, 1.0)

GAMMA_GAS = 1.0 / (G_GAS - 1.0)
GAMMA_SLOPE = 1.0 / (G_LIQUID - 1.0) - GAMMA_GAS
STIFF_GAS = G_GAS * PI_GAS / (G_GAS - 1.0)
STIFF_SLOPE = G_LIQUID * PI_LIQUID / (G_LIQUID - 1.0) - STIFF_GAS

TILES = 16
ROWS = 8
LANES = 128
GHOST = 3
RADIAL_TILES = 1
AXIAL_TILES = 3


def mixture(fraction):
    gamma_sum = GAMMA_GAS + GAMMA_SLOPE * fraction
    stiff_sum = STIFF_SLOPE * fraction
    if STIFF_GAS != 0.0:
        stiff_sum = stiff_sum + STIFF_GAS
    return gamma_sum, stiff_sum


def initial_cells(labels, jitter):
    def lookup(table):
        return jnp.where(labels == 0, table[0], jnp.where(labels == 1, table[1], table[2]))

    fraction = lookup(ALPHA_TABLE)
    part_one = fraction * lookup(LIQUID_TABLE) * jitter
    part_two = (1.0 - fraction) * lookup(GAS_TABLE) * jitter
    speed = lookup(VELOCITY_TABLE)
    pressure = lookup(PRESSURE_TABLE) * jitter
    return part_one, part_two, speed, pressure, fraction


def ambient_cell():
    fraction = ALPHA_TABLE[0]
    part_one = fraction * LIQUID_TABLE[0]
    part_two = (1.0 - fraction) * GAS_TABLE[0]
    density = part_one + part_two
    speed, pressure = VELOCITY_TABLE[0], PRESSURE_TABLE[0]
    gamma_sum, stiff_sum = mixture(fraction)
    energy = gamma_sum * pressure + stiff_sum + 0.5 * density * speed * speed
    return part_one, part_two, density * speed, 0.0, energy, fraction


def celerity_of(density, pressure, gamma_sum, stiff_sum):
    top = gamma_sum * pressure + stiff_sum + pressure
    return top * lax.rsqrt(top * (gamma_sum * density))


def weno_terms(ea, eb, ec, ed, da, db, dc, ta, tb, tc, ga, gb):
    smooth_zero = ta + eb * (eb + da)
    smooth_one = tb + eb * ec
    smooth_two = tc + ec * (ec - dc)
    square_zero = smooth_zero * smooth_zero
    square_one = smooth_one * smooth_one
    square_two = smooth_two * smooth_two
    weight_zero = square_one * square_two
    weight_one = square_zero * square_two
    weight_two = square_zero * square_one
    low = weight_zero * ga
    high = weight_two * gb
    both = low + high
    twice = both + both
    common = 6.0 * weight_one + (weight_zero + weight_two)
    upper = (twice + high) / (common + (weight_two + weight_two))
    lower = (twice + low) / (common + (weight_zero + weight_zero))
    return upper, lower


def weno_cell(cells):
    m2, m1, c, p1, p2 = cells
    ea, eb, ec, ed = m1 - m2, c - m1, p1 - c, p2 - p1
    da, db, dc = eb - ea, ec - eb, ed - ec
    ta, tb, tc = (d * (d * (4.0 / 3.0)) + WENO_EPS for d in (da, db, dc))
    qa, qb, qc = (d * (1.0 / 6.0) for d in (da, db, dc))
    upper, lower = weno_terms(ea, eb, ec, ed, da, db, dc, ta, tb, tc, qb - qa, qc - qb)
    base = c + (qb + qb)
    return base + 0.5 * eb - upper, base - 0.5 * ec + lower


def weno_run(w, count):
    e = w[1:] - w[:-1]
    d = e[1:] - e[:-1]
    t = d * (d * (4.0 / 3.0)) + WENO_EPS
    q = d * (1.0 / 6.0)
    g = q[1:] - q[:-1]
    n = count
    upper, lower = weno_terms(
        e[:n], e[1 : n + 1], e[2 : n + 2], e[3:], d[:n], d[1 : n + 1], d[2:], t[:n], t[1 : n + 1], t[2:], g[:n], g[1:]
    )
    middle = q[1 : n + 1]
    base = w[2 : n + 2] + (middle + middle)
    return base + 0.5 * e[1 : n + 1] - upper, base - 0.5 * e[2 : n + 2] + lower


def hllc(left, right, normal):
    tangent = 5 - normal

    def side(state):
        density = state[0] + state[1]
        gamma_sum, stiff_sum = mixture(state[5])
        inner = gamma_sum * state[4] + stiff_sum
        top = inner + state[4]
        return density, inner, top * lax.rsqrt(top * (gamma_sum * density))

    rho_l, inner_l, c_l = side(left)
    rho_r, inner_r, c_r = side(right)
    n_l, n_r, p_l, p_r = left[normal], right[normal], left[4], right[4]
    low = jnp.minimum(n_l - c_l, n_r - c_r)
    high = jnp.maximum(n_l + c_l, n_r + c_r)
    mass_l = rho_l * (low - n_l)
    mass_r = rho_r * (high - n_r)
    star = (p_r - p_l + mass_l * n_l - mass_r * n_r) / (mass_l - mass_r)
    forward = star >= 0.0
    outer_left = low >= 0.0
    pick = jnp.logical_or(outer_left, forward)

    def chosen(a, b):
        return jnp.where(pick, a, b)

    q_one, q_two = chosen(left[0], right[0]), chosen(left[1], right[1])
    n, t, p = chosen(n_l, n_r), chosen(left[tangent], right[tangent]), chosen(p_l, p_r)
    wave, mass, inner = chosen(low, high), chosen(mass_l, mass_r), chosen(inner_l, inner_r)
    rho = q_one + q_two
    energy = inner + 0.5 * rho * (n * n + t * t)
    plain = jnp.logical_or(outer_left, jnp.logical_and(jnp.logical_not(pick), high < 0.0))
    inverse = 1.0 / (wave - star)
    factor = (wave - n) * inverse
    jump = star - n
    star_energy = factor * energy + jump * (rho * factor * star + p * inverse)
    star_pressure = p + mass * jump
    speed = jnp.where(plain, n, star)
    scaled = jnp.where(plain, n, factor * star)
    energy = jnp.where(plain, energy, star_energy)
    p = jnp.where(plain, p, star_pressure)
    carried = rho * scaled
    along = carried * speed + p
    across = carried * t
    moments = (along, across) if normal == 2 else (across, along)
    fraction = star * jnp.where(forward, left[5], right[5])
    return [q_one * scaled, q_two * scaled, *moments, (energy + p) * speed, fraction, star]


def kernel(
    sizes,
    labels_hbm,
    jitter_hbm,
    out_ref,
    steps_ref,
    own_labels,
    own_jitter,
    labels,
    jitter,
    cells,
    fields,
    base,
    rate,
    upper,
    lower,
    packed,
    turned,
    strip,
    strip_rate,
    edge,
    dt_ref,
    send_axial,
    send_radial,
    recv_axial,
    recv_radial,
    max_first,
    max_second,
    got_first,
    got_second,
    local_sem,
    shift_send,
    shift_recv,
    halo_send,
    halo_recv,
    first_send,
    first_recv,
    second_send,
    second_recv,
):
    z_size, x_size, core_size, rad_size = sizes
    ax_size = z_size * x_size * core_size
    ax, rad = lax.axis_index("ax"), lax.axis_index("rad")
    core = lax.rem(ax, core_size)
    x = lax.rem(lax.div(ax, core_size), x_size)
    z = lax.div(ax, core_size * x_size)

    def at(z, x, core, rad):
        return ((z * x_size + x) * core_size + core, rad)

    first_group = [
        at(lax.rem(z + dz, z_size), x, lax.rem(core + dc, core_size), rad)
        for dz in range(z_size)
        for dc in range(core_size)
        if (dz, dc) != (0, 0)
    ]
    second_group = [
        at(z, lax.rem(x + dx, x_size), core, lax.rem(rad + dr, rad_size))
        for dx in range(x_size)
        for dr in range(rad_size)
        if (dx, dr) != (0, 0)
    ]
    ax_next = (lax.rem(ax + 1, ax_size), rad)
    ax_last = (lax.rem(ax + ax_size - 1, ax_size), rad)
    rad_next = (ax, lax.rem(rad + 1, rad_size))
    rad_last = (ax, lax.rem(rad + rad_size - 1, rad_size))

    block_first = ax == ax_size - 1
    block_last = ax == ax_size - 2
    wall = rad == 0
    outer = rad == rad_size - 1

    lane = lax.broadcasted_iota(jnp.int32, (ROWS, LANES), 1)
    row = lax.broadcasted_iota(jnp.int32, (ROWS, LANES), 0)

    copies = [
        pltpu.make_async_copy(labels_hbm, own_labels, local_sem.at[0]),
        pltpu.make_async_copy(jitter_hbm, own_jitter, local_sem.at[1]),
    ]
    for copy in copies:
        copy.start()
    barrier = pltpu.get_barrier_semaphore()
    greeted = first_group + second_group + [ax_next, ax_last]
    for device in greeted:
        pl.semaphore_signal(barrier, inc=1, device_id=device, device_id_type=MESH)
    for copy in copies:
        copy.wait()

    def first_copies(step):
        return [
            pltpu.make_async_remote_copy(
                src_ref=max_first.at[step],
                dst_ref=got_first.at[step, i],
                send_sem=first_send.at[step, i],
                recv_sem=first_recv.at[step, i],
                device_id=device,
                device_id_type=MESH,
            )
            for i, device in enumerate(first_group)
        ]

    def second_copies(step):
        return [
            pltpu.make_async_remote_copy(
                src_ref=max_second.at[step],
                dst_ref=got_second.at[step, i],
                send_sem=second_send.at[step, i],
                recv_sem=second_recv.at[step, i],
                device_id=device,
                device_id_type=MESH,
            )
            for i, device in enumerate(second_group)
        ]

    def halo_copies(stage):
        pairs = [
            (send_axial.at[1], recv_axial.at[stage, 0], ax_next),
            (send_axial.at[0], recv_axial.at[stage, 1], ax_last),
            (send_radial.at[1], recv_radial.at[stage, 0], rad_next),
            (send_radial.at[0], recv_radial.at[stage, 1], rad_last),
        ]
        return [
            pltpu.make_async_remote_copy(
                src_ref=source,
                dst_ref=target,
                send_sem=halo_send.at[stage, i],
                recv_sem=halo_recv.at[stage, i],
                device_id=device,
                device_id_type=MESH,
            )
            for i, (source, target, device) in enumerate(pairs)
        ]

    def own_speed(t, most):
        part_one, part_two, speed, pressure, fraction = initial_cells(
            own_labels[pl.ds(t * ROWS, ROWS), :], own_jitter[pl.ds(t * ROWS, ROWS), :]
        )
        celerity = celerity_of(part_one + part_two, pressure, *mixture(fraction))
        return jnp.maximum(most, jnp.abs(speed) + celerity)

    most = lax.fori_loop(0, TILES, own_speed, jnp.zeros((ROWS, LANES), jnp.float32))
    max_first[0] = jnp.max(most, axis=0, keepdims=True)

    pl.semaphore_wait(barrier, len(greeted))
    for copy in first_copies(0):
        copy.start()
    shifts = [
        pltpu.make_async_remote_copy(
            src_ref=source,
            dst_ref=target,
            send_sem=shift_send.at[i],
            recv_sem=shift_recv.at[i],
            device_id=ax_last,
            device_id_type=MESH,
        )
        for i, (source, target) in enumerate(((labels_hbm, labels), (jitter_hbm, jitter)))
    ]
    for copy in shifts:
        copy.start()
    for copy in shifts:
        copy.wait()

    def start_cells(t, carry):
        rows = pl.ds(t, ROWS, stride=TILES)
        part_one, part_two, speed, pressure, fraction = initial_cells(labels[rows, :], jitter[rows, :])
        density = part_one + part_two
        gamma_sum, stiff_sum = mixture(fraction)
        still = jnp.zeros_like(density)
        energy = gamma_sum * pressure + stiff_sum + 0.5 * density * speed * speed
        for i, value in enumerate((part_one, part_two, density * speed, still, energy, fraction)):
            fields[i, t] = value
            base[i, t] = value
        for i, value in enumerate((part_one, part_two, speed, still, pressure, fraction)):
            cells[i, GHOST + t] = value
        return carry

    lax.fori_loop(0, TILES, start_cells, 0)

    radius = (rad * LANES + lane).astype(jnp.float32) + 0.5

    def stage_body(stage, carry):
        step = lax.div(stage, 3)
        section = stage - 3 * step
        halos = halo_copies(stage)

        for i in range(6):
            for k in range(GHOST):
                send_axial[0, 3 * i + k] = cells[i, GHOST + k, 0:1, :]
                send_axial[1, 3 * i + k] = cells[i, TILES + k, ROWS - 1 : ROWS, :]
        halos[0].start()
        halos[1].start()

        def pack(t, carry):
            total = pltpu.roll(cells[0, GHOST + t], (0 - 122) % LANES, 1)
            for i in range(1, 6):
                rolled = pltpu.roll(cells[i, GHOST + t], (12 * i - 122) % LANES, 1)
                total = jnp.where(lane >= 12 * i, rolled, total)
            packed[t] = total
            return carry

        lax.fori_loop(0, TILES, pack, 0)
        turned[...] = packed[...].reshape(LANES, LANES).T
        for i in range(6):
            send_radial[1, 3 * i : 3 * i + 3, :] = turned[12 * i + 3 : 12 * i + 6, :]
            send_radial[0, 3 * i : 3 * i + 3, :] = turned[12 * i + 6 : 12 * i + 9, :]
        halos[2].start()
        halos[3].start()
        for i in range(6):
            strip[i, pl.ds(1, 6, stride=2), :] = turned[12 * i : 12 * i + 6, :]
            strip[i, pl.ds(6, 6, stride=2), :] = turned[12 * i + 6 : 12 * i + 12, :]

        def radial(r, carry):
            tiles = pl.ds(GHOST + r * RADIAL_TILES, RADIAL_TILES)
            left, right = [], []
            for i in range(6):
                w = cells[i, tiles]
                around = [pltpu.roll(w, shift, 2) if shift else w for shift in (2, 1, 0, LANES - 1, LANES - 2)]
                up, down = weno_cell(around)
                left.append(pltpu.roll(up, 1, 2))
                right.append(down)
            flux = hllc(left, right, 3)
            change = [value - pltpu.roll(value, LANES - 1, 2) for value in flux]
            change[5] = change[5] - cells[5, tiles] * change[6]
            for i in range(6):
                rate[i, pl.ds(r * RADIAL_TILES, RADIAL_TILES)] = change[i]
            return carry

        lax.fori_loop(0, TILES // RADIAL_TILES, radial, 0)

        @pl.when(section == 0)
        def _():
            sends = first_copies(step)
            for copy in sends:
                copy.wait_recv()
            max_second[step] = jnp.maximum(max_first[step], jnp.max(got_first[step], axis=0))
            for copy in second_copies(step):
                copy.start()

        halos[0].wait_recv()
        halos[1].wait_recv()
        for i in range(6):
            first_row = cells[i, GHOST, 0:1, :]
            last_row = cells[i, GHOST + TILES - 1, ROWS - 1 : ROWS, :]
            for k in range(GHOST):
                before = jnp.where(block_first, first_row, recv_axial[stage, 0, 3 * i + k])
                after = jnp.where(block_last, last_row, recv_axial[stage, 1, 3 * i + k])
                cells[i, k] = jnp.where(row == 0, before, pltpu.roll(cells[i, TILES + k], 1, 0))
                cells[i, GHOST + TILES + k] = jnp.where(
                    row == ROWS - 1, after, pltpu.roll(cells[i, GHOST + k], ROWS - 1, 0)
                )

        def axial_states(i, carry):
            def chunk(r, carry):
                w = cells[i, pl.ds(r * AXIAL_TILES, AXIAL_TILES + 4)]
                up, down = weno_run(w, AXIAL_TILES)
                upper[i, pl.ds(r * AXIAL_TILES, AXIAL_TILES)] = up
                lower[i, pl.ds(r * AXIAL_TILES, AXIAL_TILES)] = down
                return carry

            return lax.fori_loop(0, (TILES + 2) // AXIAL_TILES, chunk, carry)

        lax.fori_loop(0, 6, axial_states, 0)

        halos[2].wait_recv()
        halos[3].wait_recv()
        for i in range(6):
            sign = -1.0 if i == 3 else 1.0
            for k in range(GHOST):
                mirror = strip[i, 2 * (5 - k) : 2 * (5 - k) + 1, :] * sign
                strip[i, 2 * k : 2 * k + 1, :] = jnp.where(
                    wall, mirror, recv_radial[stage, 0, 3 * i + k : 3 * i + k + 1, :]
                )
                nearest = strip[i, 11:12, :]
                strip[i, 2 * k + 13 : 2 * k + 14, :] = jnp.where(
                    outer, nearest, recv_radial[stage, 1, 3 * i + k : 3 * i + k + 1, :]
                )
        left, right = [], []
        for i in range(6):
            w = [strip[i, 2 * k : 2 * k + 8, :] for k in range(6)]
            left.append(weno_cell(w[:5])[0])
            right.append(weno_cell(w[1:])[1])
        flux = hllc(left, right, 3)
        change = [value - pltpu.roll(value, ROWS - 2, 0) for value in flux]
        change[5] = change[5] - strip[5, 6:14, :] * change[6]
        for i in range(6):
            strip_rate[i] = change[i]
        for i in range(6):
            turned[8 * i : 8 * i + 3, :] = strip_rate[i, pl.ds(1, 3, stride=2), :]
            turned[8 * i + 3 : 8 * i + 6, :] = strip_rate[i, pl.ds(0, 3, stride=2), :]
        edge[...] = turned[...].T.reshape(TILES, ROWS, LANES)

        def axial_flux(f):
            return hllc([upper[i, f] for i in range(6)], [lower[i, f + 1] for i in range(6)], 2)

        def axial(t, carry):
            below = carry
            above = axial_flux(t + 1)
            at_edge = jnp.logical_or(lane < GHOST, lane >= LANES - GHOST)
            strips = edge[t]
            q_one, q_two, u, v, p, a = (cells[i, GHOST + t] for i in range(6))
            over = v / radius
            carried = (q_one + q_two) * over
            source = (q_one * over, q_two * over, u * carried, v * carried, (fields[4, t] + p) * over)
            for i in range(6):
                rim = pltpu.roll(strips, (LANES - GHOST - 8 * i) % LANES, 1)
                radial_part = jnp.where(at_edge, rim, rate[i, t])
                axial_part = below[i] - above[i]
                last = -source[i] if i < 5 else a * (above[6] - below[6])
                rate[i, t] = radial_part + axial_part + last
            return tuple(above)

        lax.fori_loop(0, TILES, axial, tuple(axial_flux(0)))

        @pl.when(section == 0)
        def _():
            sends = second_copies(step)
            for copy in sends:
                copy.wait_recv()
            top = jnp.maximum(max_second[step], jnp.max(got_second[step], axis=0))
            dt = CFL_NUMBER / jnp.broadcast_to(jnp.max(top, axis=1, keepdims=True), (ROWS, LANES))
            dt_ref[...] = dt
            steps_ref[step] = jnp.max(dt)
            for copy in sends:
                copy.wait_send()
            for copy in first_copies(step):
                copy.wait_send()

        for copy in halos:
            copy.wait_send()

        third = jnp.float32(1.0 / 3.0)
        keep = jnp.where(section == 0, 0.0, jnp.where(section == 1, 0.75, third))
        take = jnp.where(section == 0, 1.0, jnp.where(section == 1, 0.25, jnp.float32(2.0 / 3.0)))
        closing = section == 2

        def update(t, most):
            dt = dt_ref[...]
            new = []
            for i in range(6):
                value = keep * base[i, t] + take * (fields[i, t] + dt * rate[i, t])
                fields[i, t] = value
                base[i, t] = jnp.where(closing, value, base[i, t])
                new.append(value)
            density = new[0] + new[1]
            gamma_sum, stiff_sum = mixture(new[5])
            inverse = 1.0 / (density * gamma_sum)
            per_density = inverse * gamma_sum
            u = new[2] * per_density
            v = new[3] * per_density
            p = (new[4] - 0.5 * (new[2] * u + new[3] * v) - stiff_sum) * (inverse * density)
            for i, value in enumerate((new[0], new[1], u, v, p, new[5])):
                cells[i, GHOST + t] = value
            speed = jnp.abs(u) + jnp.abs(v) + celerity_of(density, p, gamma_sum, stiff_sum)
            return jnp.maximum(most, speed)

        most = lax.fori_loop(0, TILES, update, jnp.zeros((ROWS, LANES), jnp.float32))

        @pl.when(jnp.logical_and(closing, step < STEPS - 1))
        def _():
            max_first[step + 1] = jnp.max(most, axis=0, keepdims=True)
            for copy in first_copies(step + 1):
                copy.start()

        return carry

    lax.fori_loop(0, STAGES, stage_body, 0)

    def finish(t, carry):
        for i, value in enumerate(ambient_cell()):
            out_ref[i, pl.ds(t, ROWS, stride=TILES), :] = jnp.where(block_first, jnp.float32(value), fields[i, t])
        return carry

    lax.fori_loop(0, TILES, finish, 0)


def solution(mesh):
    ax_size, rad_size = mesh.shape["ax"], mesh.shape["rad"]
    sizes = (ax_size // (2 * X_CHIPS), X_CHIPS, 2, rad_size)
    first = sizes[0] * sizes[2] - 1
    second = sizes[1] * sizes[3] - 1

    def shards(labels, jitter):
        block = labels.shape
        f32 = jnp.float32
        tile = (TILES, ROWS, LANES)
        dma = pltpu.SemaphoreType.DMA
        return pl.pallas_call(
            functools.partial(kernel, sizes),
            out_shape=(jax.ShapeDtypeStruct((6, *block), f32), jax.ShapeDtypeStruct((STEPS,), f32)),
            in_specs=[pl.BlockSpec(memory_space=pl.ANY)] * 2,
            out_specs=(pl.BlockSpec(memory_space=pltpu.VMEM), pl.BlockSpec(memory_space=pltpu.SMEM)),
            scratch_shapes=[
                pltpu.VMEM(block, jnp.int32),
                pltpu.VMEM(block, f32),
                pltpu.VMEM(block, jnp.int32),
                pltpu.VMEM(block, f32),
                pltpu.VMEM((6, TILES + 2 * GHOST, ROWS, LANES), f32),
                pltpu.VMEM((6, *tile), f32),
                pltpu.VMEM((6, *tile), f32),
                pltpu.VMEM((6, *tile), f32),
                pltpu.VMEM((6, TILES + 2, ROWS, LANES), f32),
                pltpu.VMEM((6, TILES + 2, ROWS, LANES), f32),
                pltpu.VMEM(tile, f32),
                pltpu.VMEM((LANES, LANES), f32),
                pltpu.VMEM((6, 24, LANES), f32),
                pltpu.VMEM((6, ROWS, LANES), f32),
                pltpu.VMEM(tile, f32),
                pltpu.VMEM((ROWS, LANES), f32),
                pltpu.VMEM((2, 18, 1, LANES), f32),
                pltpu.VMEM((2, 24, LANES), f32),
                pltpu.VMEM((STAGES, 2, 18, 1, LANES), f32),
                pltpu.VMEM((STAGES, 2, 24, LANES), f32),
                pltpu.VMEM((STEPS, 1, LANES), f32),
                pltpu.VMEM((STEPS, 1, LANES), f32),
                pltpu.VMEM((STEPS, first, 1, LANES), f32),
                pltpu.VMEM((STEPS, second, 1, LANES), f32),
                dma((2,)),
                dma((2,)),
                dma((2,)),
                dma((STAGES, 4)),
                dma((STAGES, 4)),
                dma((STEPS, first)),
                dma((STEPS, first)),
                dma((STEPS, second)),
                dma((STEPS, second)),
            ],
            compiler_params=pltpu.CompilerParams(collective_id=0, has_side_effects=True),
        )(labels, jitter)

    return jax.shard_map(
        shards, mesh=mesh, in_specs=(P("ax", "rad"),) * 2, out_specs=(P(None, "ax", "rad"), P()), check_vma=False
    )
```

time: 340 us -> 111 us (0.33)
  the two profiles are of different devices: /device:TPU:41 before, /device:TPU:1 now
where the time goes in v1:
time: 111 us
  Pallas kernels  108 us (97%)
  local copies, waits for them, and re-layouts  2.28 us (2%)
    pallas_call x1, Pallas kernels, shards(): pl.pallas_call(functools.partial(kernel, sizes), out_shape=(jax.ShapeDtyp...  108 us
    unnamed x4, local copies, waits for them, and re-layouts  2.28 us

profile of v1, /device:TPU:1, one launch (start us, length us, event | category | flops | bytes accessed | tf_op | source)
XLA Modules:
  0.0 110.7 jit_solution(11068012229276173432)
XLA Ops:
  0.6 107.8 %shard_map.41 = (f32[6,128,128]{2,1,0:T(8,128)}, f32[3]{0:T(128)}) custom-call(s32[128,128]{1,0:T(8,128)} %labels_hbm.1, f32[128,128]{1,0:T(8,128)} %jitter_hbm.1), custom_call_target="tpu_custom_call" | custom-call | tf_op jit(solution)/shard_map/pallas_call | solution.py:557
  108.4 0.0 copy-start
  108.4 1.8 %copy.6 = f32[6,128,128]{2,1,0:T(8,128)} copy(f32[6,128,128]{2,1,0:T(8,128)} %get-tuple-element.4) | data formatting | bytes 786432
  110.2 0.0 copy-done
  110.2 0.5 copy.7
Async XLA Ops:
  108.4 1.8 %copy-start = (f32[3]{0:T(128)S(1)}, f32[3]{0:T(128)}, u32[]{:S(2)}) copy-start(f32[3]{0:T(128)} %get-tuple-element.5) | copy-start | bytes 40

commit v2 on v1

--- a/solution.py
+++ b/solution.py
@@ -34,8 +34,9 @@
 ROWS = 8
 LANES = 128
 GHOST = 3
-RADIAL_TILES = 1
-AXIAL_TILES = 3
+FACES = 3
+UPDATES = 2
+INNER = 12
 
 
 def mixture(fraction):
@@ -92,17 +93,6 @@
     upper = (twice + high) / (common + (weight_two + weight_two))
     lower = (twice + low) / (common + (weight_zero + weight_zero))
     return upper, lower
-
-
-def weno_cell(cells):
-    m2, m1, c, p1, p2 = cells
-    ea, eb, ec, ed = m1 - m2, c - m1, p1 - c, p2 - p1
-    da, db, dc = eb - ea, ec - eb, ed - ec
-    ta, tb, tc = (d * (d * (4.0 / 3.0)) + WENO_EPS for d in (da, db, dc))
-    qa, qb, qc = (d * (1.0 / 6.0) for d in (da, db, dc))
-    upper, lower = weno_terms(ea, eb, ec, ed, da, db, dc, ta, tb, tc, qb - qa, qc - qb)
-    base = c + (qb + qb)
-    return base + 0.5 * eb - upper, base - 0.5 * ec + lower
 
 
 def weno_run(w, count):
@@ -178,17 +168,15 @@
     own_jitter,
     labels,
     jitter,
-    cells,
+    axial_cells,
+    radial_cells,
     fields,
     base,
-    rate,
     upper,
     lower,
-    packed,
+    axial_rate,
+    radial_rate,
     turned,
-    strip,
-    strip_rate,
-    edge,
     dt_ref,
     send_axial,
     send_radial,
@@ -330,9 +318,14 @@
     for copy in shifts:
         copy.wait()
 
+    to_lanes = (lane % ROWS) * TILES + lane // ROWS
+    from_lanes = (lane % TILES) * ROWS + lane // TILES
+
     def start_cells(t, carry):
         rows = pl.ds(t, ROWS, stride=TILES)
-        part_one, part_two, speed, pressure, fraction = initial_cells(labels[rows, :], jitter[rows, :])
+        part_one, part_two, speed, pressure, fraction = initial_cells(
+            jnp.take_along_axis(labels[rows, :], to_lanes, axis=1), jnp.take_along_axis(jitter[rows, :], to_lanes, axis=1)
+        )
         density = part_one + part_two
         gamma_sum, stiff_sum = mixture(fraction)
         still = jnp.zeros_like(density)
@@ -341,61 +334,97 @@
             fields[i, t] = value
             base[i, t] = value
         for i, value in enumerate((part_one, part_two, speed, still, pressure, fraction)):
-            cells[i, GHOST + t] = value
+            axial_cells[i, GHOST + t] = value
         return carry
 
     lax.fori_loop(0, TILES, start_cells, 0)
 
-    radius = (rad * LANES + lane).astype(jnp.float32) + 0.5
+    radius = (rad * LANES + to_lanes).astype(jnp.float32) + 0.5
+    per_radius = 1.0 / radius
+
+    def take_rims(cells, send):
+        for i in range(6):
+            for k in range(GHOST):
+                send[0, 3 * i + k] = cells[i, GHOST + k, 0:1, :]
+                send[1, 3 * i + k] = cells[i, TILES + k, ROWS - 1 : ROWS, :]
+
+    def ghosts(cells, recv, stage, at_low, at_high, mirrored):
+        for i in range(6):
+            for k in range(GHOST):
+                if mirrored:
+                    low = cells[i, 2 * GHOST - 1 - k, 0:1, :]
+                    if i == 3:
+                        low = -low
+                else:
+                    low = cells[i, GHOST, 0:1, :]
+                high = cells[i, GHOST + TILES - 1, ROWS - 1 : ROWS, :]
+                before = jnp.where(at_low, low, recv[stage, 0, 3 * i + k])
+                after = jnp.where(at_high, high, recv[stage, 1, 3 * i + k])
+                cells[i, k] = jnp.where(row == 0, before, pltpu.roll(cells[i, TILES + k], 1, 0))
+                cells[i, GHOST + TILES + k] = jnp.where(
+                    row == ROWS - 1, after, pltpu.roll(cells[i, GHOST + k], ROWS - 1, 0)
+                )
+
+    def states(cells, which, i, first, count):
+        up, down = weno_run(cells[i, first : first + count + 4], count)
+        upper[which, i, first : first + count] = up
+        lower[which, i, first : first + count] = down
+
+    def rim_states(cells, which):
+        def one(i, carry):
+            states(cells, which, i, 0, 3)
+            states(cells, which, i, 15, 3)
+            return carry
+
+        lax.fori_loop(0, 6, one, 0)
+
+    def faces(cells, which, rate, normal):
+        def some(r, below):
+            for k in range(FACES):
+                f = r * FACES + k
+                above = hllc([upper[which, i, f] for i in range(6)], [lower[which, i, f + 1] for i in range(6)], normal)
+                change = [b - a for b, a in zip(below, above)]
+                change[5] = change[5] - cells[5, f + 2] * change[6]
+                for i in range(6):
+                    rate[i, f] = change[i]
+                below = tuple(above)
+            return below
+
+        lax.fori_loop(0, (TILES + 2) // FACES, some, (jnp.zeros((ROWS, LANES), jnp.float32),) * 7)
 
     def stage_body(stage, carry):
         step = lax.div(stage, 3)
         section = stage - 3 * step
         halos = halo_copies(stage)
 
-        for i in range(6):
-            for k in range(GHOST):
-                send_axial[0, 3 * i + k] = cells[i, GHOST + k, 0:1, :]
-                send_axial[1, 3 * i + k] = cells[i, TILES + k, ROWS - 1 : ROWS, :]
+        take_rims(axial_cells, send_axial)
         halos[0].start()
         halos[1].start()
 
-        def pack(t, carry):
-            total = pltpu.roll(cells[0, GHOST + t], (0 - 122) % LANES, 1)
-            for i in range(1, 6):
-                rolled = pltpu.roll(cells[i, GHOST + t], (12 * i - 122) % LANES, 1)
-                total = jnp.where(lane >= 12 * i, rolled, total)
-            packed[t] = total
+        def turn(i, carry):
+            block = axial_cells[i, GHOST : GHOST + TILES].reshape(LANES, LANES)
+            radial_cells[i, GHOST : GHOST + TILES] = block.T.reshape(TILES, ROWS, LANES)
+            for first in range(3, 15, INNER):
+                states(axial_cells, 0, i, first, INNER)
             return carry
 
-        lax.fori_loop(0, TILES, pack, 0)
-        turned[...] = packed[...].reshape(LANES, LANES).T
-        for i in range(6):
-            send_radial[1, 3 * i : 3 * i + 3, :] = turned[12 * i + 3 : 12 * i + 6, :]
-            send_radial[0, 3 * i : 3 * i + 3, :] = turned[12 * i + 6 : 12 * i + 9, :]
+        lax.fori_loop(0, 6, turn, 0)
+        take_rims(radial_cells, send_radial)
         halos[2].start()
         halos[3].start()
-        for i in range(6):
-            strip[i, pl.ds(1, 6, stride=2), :] = turned[12 * i : 12 * i + 6, :]
-            strip[i, pl.ds(6, 6, stride=2), :] = turned[12 * i + 6 : 12 * i + 12, :]
-
-        def radial(r, carry):
-            tiles = pl.ds(GHOST + r * RADIAL_TILES, RADIAL_TILES)
-            left, right = [], []
-            for i in range(6):
-                w = cells[i, tiles]
-                around = [pltpu.roll(w, shift, 2) if shift else w for shift in (2, 1, 0, LANES - 1, LANES - 2)]
-                up, down = weno_cell(around)
-                left.append(pltpu.roll(up, 1, 2))
-                right.append(down)
-            flux = hllc(left, right, 3)
-            change = [value - pltpu.roll(value, LANES - 1, 2) for value in flux]
-            change[5] = change[5] - cells[5, tiles] * change[6]
-            for i in range(6):
-                rate[i, pl.ds(r * RADIAL_TILES, RADIAL_TILES)] = change[i]
+
+        def inner(i, carry):
+            for first in range(3, 15, INNER):
+                states(radial_cells, 1, i, first, INNER)
             return carry
 
-        lax.fori_loop(0, TILES // RADIAL_TILES, radial, 0)
+        lax.fori_loop(0, 6, inner, 0)
+
+        halos[0].wait_recv()
+        halos[1].wait_recv()
+        ghosts(axial_cells, recv_axial, stage, block_first, block_last, False)
+        rim_states(axial_cells, 0)
+        faces(axial_cells, 0, axial_rate, 2)
 
         @pl.when(section == 0)
         def _():
@@ -406,80 +435,18 @@
             for copy in second_copies(step):
                 copy.start()
 
-        halos[0].wait_recv()
-        halos[1].wait_recv()
-        for i in range(6):
-            first_row = cells[i, GHOST, 0:1, :]
-            last_row = cells[i, GHOST + TILES - 1, ROWS - 1 : ROWS, :]
-            for k in range(GHOST):
-                before = jnp.where(block_first, first_row, recv_axial[stage, 0, 3 * i + k])
-                after = jnp.where(block_last, last_row, recv_axial[stage, 1, 3 * i + k])
-                cells[i, k] = jnp.where(row == 0, before, pltpu.roll(cells[i, TILES + k], 1, 0))
-                cells[i, GHOST + TILES + k] = jnp.where(
-                    row == ROWS - 1, after, pltpu.roll(cells[i, GHOST + k], ROWS - 1, 0)
-                )
-
-        def axial_states(i, carry):
-            def chunk(r, carry):
-                w = cells[i, pl.ds(r * AXIAL_TILES, AXIAL_TILES + 4)]
-                up, down = weno_run(w, AXIAL_TILES)
-                upper[i, pl.ds(r * AXIAL_TILES, AXIAL_TILES)] = up
-                lower[i, pl.ds(r * AXIAL_TILES, AXIAL_TILES)] = down
-                return carry
-
-            return lax.fori_loop(0, (TILES + 2) // AXIAL_TILES, chunk, carry)
-
-        lax.fori_loop(0, 6, axial_states, 0)
-
         halos[2].wait_recv()
         halos[3].wait_recv()
-        for i in range(6):
-            sign = -1.0 if i == 3 else 1.0
-            for k in range(GHOST):
-                mirror = strip[i, 2 * (5 - k) : 2 * (5 - k) + 1, :] * sign
-                strip[i, 2 * k : 2 * k + 1, :] = jnp.where(
-                    wall, mirror, recv_radial[stage, 0, 3 * i + k : 3 * i + k + 1, :]
-                )
-                nearest = strip[i, 11:12, :]
-                strip[i, 2 * k + 13 : 2 * k + 14, :] = jnp.where(
-                    outer, nearest, recv_radial[stage, 1, 3 * i + k : 3 * i + k + 1, :]
-                )
-        left, right = [], []
-        for i in range(6):
-            w = [strip[i, 2 * k : 2 * k + 8, :] for k in range(6)]
-            left.append(weno_cell(w[:5])[0])
-            right.append(weno_cell(w[1:])[1])
-        flux = hllc(left, right, 3)
-        change = [value - pltpu.roll(value, ROWS - 2, 0) for value in flux]
-        change[5] = change[5] - strip[5, 6:14, :] * change[6]
-        for i in range(6):
-            strip_rate[i] = change[i]
-        for i in range(6):
-            turned[8 * i : 8 * i + 3, :] = strip_rate[i, pl.ds(1, 3, stride=2), :]
-            turned[8 * i + 3 : 8 * i + 6, :] = strip_rate[i, pl.ds(0, 3, stride=2), :]
-        edge[...] = turned[...].T.reshape(TILES, ROWS, LANES)
-
-        def axial_flux(f):
-            return hllc([upper[i, f] for i in range(6)], [lower[i, f + 1] for i in range(6)], 2)
-
-        def axial(t, carry):
-            below = carry
-            above = axial_flux(t + 1)
-            at_edge = jnp.logical_or(lane < GHOST, lane >= LANES - GHOST)
-            strips = edge[t]
-            q_one, q_two, u, v, p, a = (cells[i, GHOST + t] for i in range(6))
-            over = v / radius
-            carried = (q_one + q_two) * over
-            source = (q_one * over, q_two * over, u * carried, v * carried, (fields[4, t] + p) * over)
-            for i in range(6):
-                rim = pltpu.roll(strips, (LANES - GHOST - 8 * i) % LANES, 1)
-                radial_part = jnp.where(at_edge, rim, rate[i, t])
-                axial_part = below[i] - above[i]
-                last = -source[i] if i < 5 else a * (above[6] - below[6])
-                rate[i, t] = radial_part + axial_part + last
-            return tuple(above)
-
-        lax.fori_loop(0, TILES, axial, tuple(axial_flux(0)))
+        ghosts(radial_cells, recv_radial, stage, wall, outer, True)
+        rim_states(radial_cells, 1)
+        faces(radial_cells, 1, radial_rate, 3)
+
+        def turn_back(i, carry):
+            block = radial_rate[i, 1 : 1 + TILES].reshape(LANES, LANES)
+            turned[i] = block.T.reshape(TILES, ROWS, LANES)
+            return carry
+
+        lax.fori_loop(0, 6, turn_back, 0)
 
         @pl.when(section == 0)
         def _():
@@ -502,28 +469,40 @@
         keep = jnp.where(section == 0, 0.0, jnp.where(section == 1, 0.75, third))
         take = jnp.where(section == 0, 1.0, jnp.where(section == 1, 0.25, jnp.float32(2.0 / 3.0)))
         closing = section == 2
-
-        def update(t, most):
-            dt = dt_ref[...]
-            new = []
-            for i in range(6):
-                value = keep * base[i, t] + take * (fields[i, t] + dt * rate[i, t])
-                fields[i, t] = value
-                base[i, t] = jnp.where(closing, value, base[i, t])
-                new.append(value)
-            density = new[0] + new[1]
-            gamma_sum, stiff_sum = mixture(new[5])
-            inverse = 1.0 / (density * gamma_sum)
-            per_density = inverse * gamma_sum
-            u = new[2] * per_density
-            v = new[3] * per_density
-            p = (new[4] - 0.5 * (new[2] * u + new[3] * v) - stiff_sum) * (inverse * density)
-            for i, value in enumerate((new[0], new[1], u, v, p, new[5])):
-                cells[i, GHOST + t] = value
-            speed = jnp.abs(u) + jnp.abs(v) + celerity_of(density, p, gamma_sum, stiff_sum)
-            return jnp.maximum(most, speed)
-
-        most = lax.fori_loop(0, TILES, update, jnp.zeros((ROWS, LANES), jnp.float32))
+        dt = dt_ref[...]
+
+        def update(r, most):
+            for k in range(UPDATES):
+                t = r * UPDATES + k
+                q_one, q_two, u, v, p, a = (axial_cells[i, GHOST + t] for i in range(6))
+                old = [fields[i, t] for i in range(6)]
+                over = v * per_radius
+                carried = (q_one + q_two) * over
+                source = (q_one * over, q_two * over, u * carried, v * carried, (old[4] + p) * over)
+                new = []
+                for i in range(6):
+                    change = axial_rate[i, t + 1] + turned[i, t]
+                    if i < 5:
+                        change = change - source[i]
+                    start = base[i, t]
+                    value = keep * start + take * (old[i] + dt * change)
+                    fields[i, t] = value
+                    base[i, t] = jnp.where(closing, value, start)
+                    new.append(value)
+                density = new[0] + new[1]
+                gamma_sum, stiff_sum = mixture(new[5])
+                inverse = 1.0 / (density * gamma_sum)
+                per_density = inverse * gamma_sum
+                u = new[2] * per_density
+                v = new[3] * per_density
+                p = (new[4] - 0.5 * (new[2] * u + new[3] * v) - stiff_sum) * (inverse * density)
+                for i, value in enumerate((new[0], new[1], u, v, p, new[5])):
+                    axial_cells[i, GHOST + t] = value
+                speed = jnp.abs(u) + jnp.abs(v) + celerity_of(density, p, gamma_sum, stiff_sum)
+                most = jnp.maximum(most, speed)
+            return most
+
+        most = lax.fori_loop(0, TILES // UPDATES, update, jnp.zeros((ROWS, LANES), jnp.float32))
 
         @pl.when(jnp.logical_and(closing, step < STEPS - 1))
         def _():
@@ -537,7 +516,8 @@
 
     def finish(t, carry):
         for i, value in enumerate(ambient_cell()):
-            out_ref[i, pl.ds(t, ROWS, stride=TILES), :] = jnp.where(block_first, jnp.float32(value), fields[i, t])
+            moved = jnp.take_along_axis(fields[i, t], from_lanes, axis=1)
+            out_ref[i, pl.ds(t, ROWS, stride=TILES), :] = jnp.where(block_first, jnp.float32(value), moved)
         return carry
 
     lax.fori_loop(0, TILES, finish, 0)
@@ -565,21 +545,19 @@
                 pltpu.VMEM(block, jnp.int32),
                 pltpu.VMEM(block, f32),
                 pltpu.VMEM((6, TILES + 2 * GHOST, ROWS, LANES), f32),
+                pltpu.VMEM((6, TILES + 2 * GHOST, ROWS, LANES), f32),
                 pltpu.VMEM((6, *tile), f32),
                 pltpu.VMEM((6, *tile), f32),
-                pltpu.VMEM((6, *tile), f32),
+                pltpu.VMEM((2, 6, TILES + 3, ROWS, LANES), f32),
+                pltpu.VMEM((2, 6, TILES + 3, ROWS, LANES), f32),
                 pltpu.VMEM((6, TILES + 2, ROWS, LANES), f32),
                 pltpu.VMEM((6, TILES + 2, ROWS, LANES), f32),
-                pltpu.VMEM(tile, f32),
-                pltpu.VMEM((LANES, LANES), f32),
-                pltpu.VMEM((6, 24, LANES), f32),
-                pltpu.VMEM((6, ROWS, LANES), f32),
-                pltpu.VMEM(tile, f32),
+                pltpu.VMEM((6, *tile), f32),
                 pltpu.VMEM((ROWS, LANES), f32),
                 pltpu.VMEM((2, 18, 1, LANES), f32),
-                pltpu.VMEM((2, 24, LANES), f32),
+                pltpu.VMEM((2, 18, 1, LANES), f32),
                 pltpu.VMEM((STAGES, 2, 18, 1, LANES), f32),
-                pltpu.VMEM((STAGES, 2, 24, LANES), f32),
+                pltpu.VMEM((STAGES, 2, 18, 1, LANES), f32),
                 pltpu.VMEM((STEPS, 1, LANES), f32),
                 pltpu.VMEM((STEPS, 1, LANES), f32),
                 pltpu.VMEM((STEPS, first, 1, LANES), f32),

time: 111 us -> 87.8 us (0.79)
  Pallas kernels: 108 us -> 84.7 us
    pallas_call x1, Pallas kernels: 108 us -> 84.7 us  [shards(): pl.pallas_call(functools.partial(kernel, sizes), out_shape=(jax.ShapeDtyp...]
where the time goes in v2:
time: 87.8 us; the launch traced here: 87.7 us
  Pallas kernels  84.7 us (96%)
  local copies, waits for them, and re-layouts  2.28 us (3%)
    pallas_call x1, Pallas kernels, shards(): pl.pallas_call(functools.partial(kernel, sizes), out_shape=(jax.ShapeDtyp...  84.7 us
    unnamed x4, local copies, waits for them, and re-layouts  2.28 us

profile of v2, /device:TPU:1, one launch (start us, length us, event | category | flops | bytes accessed | tf_op | source)
XLA Modules:
  0.0 87.7 jit_solution(16115911574804529954)
XLA Ops:
  0.6 84.7 %shard_map.41 = (f32[6,128,128]{2,1,0:T(8,128)}, f32[3]{0:T(128)}) custom-call(s32[128,128]{1,0:T(8,128)} %labels_hbm.1, f32[128,128]{1,0:T(8,128)} %jitter_hbm.1), custom_call_target="tpu_custom_call" | custom-call | tf_op jit(solution)/shard_map/pallas_call | solution.py:537
  85.4 0.0 copy-start
  85.4 1.8 %copy.6 = f32[6,128,128]{2,1,0:T(8,128)} copy(f32[6,128,128]{2,1,0:T(8,128)} %get-tuple-element.4) | data formatting | bytes 786432
  87.2 0.0 copy-done
  87.2 0.5 copy.7
Async XLA Ops:
  85.4 1.8 %copy-start = (f32[3]{0:T(128)S(1)}, f32[3]{0:T(128)}, u32[]{:S(2)}) copy-start(f32[3]{0:T(128)} %get-tuple-element.5) | copy-start | bytes 40

commit v3 on v2

--- a/solution.py
+++ b/solution.py
@@ -35,8 +35,12 @@
 LANES = 128
 GHOST = 3
 FACES = 3
-UPDATES = 2
-INNER = 12
+RIMS = 3
+VMEM_BYTES = 16 * 2**20
+UPDATES = 5
+RUN = 6
+FINISHED = 4
+TURNS = 6
 
 
 def mixture(fraction):
@@ -93,6 +97,17 @@
     upper = (twice + high) / (common + (weight_two + weight_two))
     lower = (twice + low) / (common + (weight_zero + weight_zero))
     return upper, lower
+
+
+def weno_cell(cells):
+    m2, m1, c, p1, p2 = cells
+    ea, eb, ec, ed = m1 - m2, c - m1, p1 - c, p2 - p1
+    da, db, dc = eb - ea, ec - eb, ed - ec
+    ta, tb, tc = (d * (d * (4.0 / 3.0)) + WENO_EPS for d in (da, db, dc))
+    qa, qb, qc = (d * (1.0 / 6.0) for d in (da, db, dc))
+    upper, lower = weno_terms(ea, eb, ec, ed, da, db, dc, ta, tb, tc, qb - qa, qc - qb)
+    base = c + (qb + qb)
+    return base + 0.5 * eb - upper, base - 0.5 * ec + lower
 
 
 def weno_run(w, count):
@@ -162,7 +177,7 @@
     sizes,
     labels_hbm,
     jitter_hbm,
-    out_ref,
+    fields,
     steps_ref,
     own_labels,
     own_jitter,
@@ -170,13 +185,14 @@
     jitter,
     axial_cells,
     radial_cells,
-    fields,
     base,
     upper,
     lower,
     axial_rate,
     radial_rate,
     turned,
+    strip,
+    strip_rate,
     dt_ref,
     send_axial,
     send_radial,
@@ -270,7 +286,8 @@
             for i, device in enumerate(second_group)
         ]
 
-    def halo_copies(stage):
+    def halo_copies(stage, which=(0, 1, 2, 3)):
+        parity = lax.rem(stage, 2)
         pairs = [
             (send_axial.at[1], recv_axial.at[stage, 0], ax_next),
             (send_axial.at[0], recv_axial.at[stage, 1], ax_last),
@@ -281,12 +298,13 @@
             pltpu.make_async_remote_copy(
                 src_ref=source,
                 dst_ref=target,
-                send_sem=halo_send.at[stage, i],
-                recv_sem=halo_recv.at[stage, i],
+                send_sem=halo_send.at[parity, i],
+                recv_sem=halo_recv.at[parity, i],
                 device_id=device,
                 device_id_type=MESH,
             )
             for i, (source, target, device) in enumerate(pairs)
+            if i in which
         ]
 
     def own_speed(t, most):
@@ -318,9 +336,16 @@
     for copy in shifts:
         copy.wait()
 
+    def second_phase(step):
+        for copy in first_copies(step):
+            copy.wait_recv()
+        max_second[step] = jnp.maximum(max_first[step], jnp.max(got_first[step], axis=0))
+        for copy in second_copies(step):
+            copy.start()
+
+    second_phase(0)
+
     to_lanes = (lane % ROWS) * TILES + lane // ROWS
-    from_lanes = (lane % TILES) * ROWS + lane // TILES
-
     def start_cells(t, carry):
         rows = pl.ds(t, ROWS, stride=TILES)
         part_one, part_two, speed, pressure, fraction = initial_cells(
@@ -348,35 +373,61 @@
                 send[0, 3 * i + k] = cells[i, GHOST + k, 0:1, :]
                 send[1, 3 * i + k] = cells[i, TILES + k, ROWS - 1 : ROWS, :]
 
-    def ghosts(cells, recv, stage, at_low, at_high, mirrored):
+    def wrapped(cells):
         for i in range(6):
             for k in range(GHOST):
-                if mirrored:
-                    low = cells[i, 2 * GHOST - 1 - k, 0:1, :]
+                cells[i, k] = pltpu.roll(cells[i, TILES + k], 1, 0)
+                cells[i, GHOST + TILES + k] = pltpu.roll(cells[i, GHOST + k], ROWS - 1, 0)
+
+    def own_strip(cells, which):
+        for i in range(6):
+            q = {2: 3, 3: 2}.get(i, i) if which else i
+            for k in range(6):
+                strip[q, which, 2 * k + 6 : 2 * k + 7, :] = cells[i, GHOST + k, 0:1, :]
+                strip[q, which, 2 * k + 1 : 2 * k + 2, :] = cells[i, GHOST + 10 + k, ROWS - 1 : ROWS, :]
+
+    def rim_strip(recv, stage, which, at_low, at_high):
+        for i in range(6):
+            q = {2: 3, 3: 2}.get(i, i) if which else i
+            high = strip[q, which, 11:12, :]
+            for k in range(GHOST):
+                if which:
+                    low = strip[q, which, 10 - 2 * k : 11 - 2 * k, :]
                     if i == 3:
                         low = -low
                 else:
-                    low = cells[i, GHOST, 0:1, :]
-                high = cells[i, GHOST + TILES - 1, ROWS - 1 : ROWS, :]
-                before = jnp.where(at_low, low, recv[stage, 0, 3 * i + k])
-                after = jnp.where(at_high, high, recv[stage, 1, 3 * i + k])
-                cells[i, k] = jnp.where(row == 0, before, pltpu.roll(cells[i, TILES + k], 1, 0))
-                cells[i, GHOST + TILES + k] = jnp.where(
-                    row == ROWS - 1, after, pltpu.roll(cells[i, GHOST + k], ROWS - 1, 0)
-                )
-
-    def states(cells, which, i, first, count):
-        up, down = weno_run(cells[i, first : first + count + 4], count)
-        upper[which, i, first : first + count] = up
-        lower[which, i, first : first + count] = down
-
-    def rim_states(cells, which):
-        def one(i, carry):
-            states(cells, which, i, 0, 3)
-            states(cells, which, i, 15, 3)
-            return carry
-
-        lax.fori_loop(0, 6, one, 0)
+                    low = strip[q, which, 6:7, :]
+                strip[q, which, 2 * k : 2 * k + 1, :] = jnp.where(at_low, low, recv[stage, 0, 3 * i + k])
+                strip[q, which, 2 * k + 13 : 2 * k + 14, :] = jnp.where(at_high, high, recv[stage, 1, 3 * i + k])
+
+    def strip_rates():
+        left, right = [], []
+        for i in range(6):
+            w = [strip[i, :, 2 * k : 2 * k + 8, :] for k in range(6)]
+            left.append(weno_cell(w[:5])[0])
+            right.append(weno_cell(w[1:])[1])
+            if i == 5:
+                fraction = w[3]
+        flux = hllc(left, right, 2)
+        change = [value - pltpu.roll(value, ROWS - 2, 1) for value in flux]
+        change[5] = change[5] - fraction * change[6]
+        for i in range(6):
+            strip_rate[i] = change[i]
+        for i in range(6):
+            q = {2: 3, 3: 2}.get(i, i)
+            for k in range(GHOST):
+                axial_rate[i, 1 + k, 0:1, :] = strip_rate[i, 0, 2 * k : 2 * k + 1, :]
+                axial_rate[i, TILES - 2 + k, ROWS - 1 : ROWS, :] = strip_rate[i, 0, 2 * k + 1 : 2 * k + 2, :]
+                radial_rate[i, 1 + k, 0:1, :] = strip_rate[q, 1, 2 * k : 2 * k + 1, :]
+                radial_rate[i, TILES - 2 + k, ROWS - 1 : ROWS, :] = strip_rate[q, 1, 2 * k + 1 : 2 * k + 2, :]
+
+    def all_states(i, carry):
+        for which, cells in enumerate((axial_cells, radial_cells)):
+            for first in range(0, TILES + 2, RUN):
+                up, down = weno_run(cells[i, first : first + RUN + 4], RUN)
+                upper[which, i, first : first + RUN] = up
+                lower[which, i, first : first + RUN] = down
+        return carry
 
     def faces(cells, which, rate, normal):
         def some(r, below):
@@ -392,61 +443,58 @@
 
         lax.fori_loop(0, (TILES + 2) // FACES, some, (jnp.zeros((ROWS, LANES), jnp.float32),) * 7)
 
+    def send_axial_rims(stage):
+        take_rims(axial_cells, send_axial)
+        for copy in halo_copies(stage, (0, 1)):
+            copy.start()
+
+    def send_radial_rims(stage):
+        def turn(r, carry):
+            for k in range(TURNS):
+                i = r * TURNS + k
+                block = axial_cells[i, GHOST : GHOST + TILES].reshape(LANES, LANES)
+                radial_cells[i, GHOST : GHOST + TILES] = block.T.reshape(TILES, ROWS, LANES)
+            return carry
+
+        lax.fori_loop(0, 6 // TURNS, turn, 0)
+        take_rims(radial_cells, send_radial)
+        for copy in halo_copies(stage, (2, 3)):
+            copy.start()
+
+    send_axial_rims(0)
+    send_radial_rims(0)
+
     def stage_body(stage, carry):
         step = lax.div(stage, 3)
         section = stage - 3 * step
         halos = halo_copies(stage)
 
-        take_rims(axial_cells, send_axial)
-        halos[0].start()
-        halos[1].start()
-
-        def turn(i, carry):
-            block = axial_cells[i, GHOST : GHOST + TILES].reshape(LANES, LANES)
-            radial_cells[i, GHOST : GHOST + TILES] = block.T.reshape(TILES, ROWS, LANES)
-            for first in range(3, 15, INNER):
-                states(axial_cells, 0, i, first, INNER)
+        wrapped(axial_cells)
+        wrapped(radial_cells)
+        own_strip(axial_cells, 0)
+        own_strip(radial_cells, 1)
+        lax.fori_loop(0, 6, all_states, 0)
+        faces(axial_cells, 0, axial_rate, 2)
+        faces(radial_cells, 1, radial_rate, 3)
+
+        for copy in halos:
+            copy.wait_recv()
+        rim_strip(recv_axial, stage, 0, block_first, block_last)
+        rim_strip(recv_radial, stage, 1, wall, outer)
+        strip_rates()
+
+        @pl.when(jnp.logical_and(section == 0, step > 0))
+        def _():
+            second_phase(step)
+
+        def turn_back(r, carry):
+            for k in range(TURNS):
+                i = r * TURNS + k
+                block = radial_rate[i, 1 : 1 + TILES].reshape(LANES, LANES)
+                turned[i] = block.T.reshape(TILES, ROWS, LANES)
             return carry
 
-        lax.fori_loop(0, 6, turn, 0)
-        take_rims(radial_cells, send_radial)
-        halos[2].start()
-        halos[3].start()
-
-        def inner(i, carry):
-            for first in range(3, 15, INNER):
-                states(radial_cells, 1, i, first, INNER)
-            return carry
-
-        lax.fori_loop(0, 6, inner, 0)
-
-        halos[0].wait_recv()
-        halos[1].wait_recv()
-        ghosts(axial_cells, recv_axial, stage, block_first, block_last, False)
-        rim_states(axial_cells, 0)
-        faces(axial_cells, 0, axial_rate, 2)
-
-        @pl.when(section == 0)
-        def _():
-            sends = first_copies(step)
-            for copy in sends:
-                copy.wait_recv()
-            max_second[step] = jnp.maximum(max_first[step], jnp.max(got_first[step], axis=0))
-            for copy in second_copies(step):
-                copy.start()
-
-        halos[2].wait_recv()
-        halos[3].wait_recv()
-        ghosts(radial_cells, recv_radial, stage, wall, outer, True)
-        rim_states(radial_cells, 1)
-        faces(radial_cells, 1, radial_rate, 3)
-
-        def turn_back(i, carry):
-            block = radial_rate[i, 1 : 1 + TILES].reshape(LANES, LANES)
-            turned[i] = block.T.reshape(TILES, ROWS, LANES)
-            return carry
-
-        lax.fori_loop(0, 6, turn_back, 0)
+        lax.fori_loop(0, 6 // TURNS, turn_back, 0)
 
         @pl.when(section == 0)
         def _():
@@ -471,9 +519,8 @@
         closing = section == 2
         dt = dt_ref[...]
 
-        def update(r, most):
-            for k in range(UPDATES):
-                t = r * UPDATES + k
+        def update(tiles, most):
+            for t in tiles:
                 q_one, q_two, u, v, p, a = (axial_cells[i, GHOST + t] for i in range(6))
                 old = [fields[i, t] for i in range(6)]
                 over = v * per_radius
@@ -502,7 +549,23 @@
                 most = jnp.maximum(most, speed)
             return most
 
-        most = lax.fori_loop(0, TILES // UPDATES, update, jnp.zeros((ROWS, LANES), jnp.float32))
+        most = lax.fori_loop(
+            0,
+            GHOST // RIMS,
+            lambda r, m: update([base_tile + r * RIMS + k for k in range(RIMS) for base_tile in (0, TILES - GHOST)], m),
+            jnp.zeros((ROWS, LANES), jnp.float32),
+        )
+
+        @pl.when(stage < STAGES - 1)
+        def _():
+            send_axial_rims(stage + 1)
+
+        most = lax.fori_loop(
+            0,
+            (TILES - 2 * GHOST) // UPDATES,
+            lambda r, m: update([GHOST + r * UPDATES + k for k in range(UPDATES)], m),
+            most,
+        )
 
         @pl.when(jnp.logical_and(closing, step < STEPS - 1))
         def _():
@@ -510,17 +573,31 @@
             for copy in first_copies(step + 1):
                 copy.start()
 
+        @pl.when(stage < STAGES - 1)
+        def _():
+            send_radial_rims(stage + 1)
+
         return carry
 
     lax.fori_loop(0, STAGES, stage_body, 0)
 
-    def finish(t, carry):
-        for i, value in enumerate(ambient_cell()):
-            moved = jnp.take_along_axis(fields[i, t], from_lanes, axis=1)
-            out_ref[i, pl.ds(t, ROWS, stride=TILES), :] = jnp.where(block_first, jnp.float32(value), moved)
+
+def finish(ax_size, fields, steps, out_ref, steps_ref):
+    outside = lax.axis_index("ax") == ax_size - 1
+    lane = lax.broadcasted_iota(jnp.int32, (ROWS, LANES), 1)
+    from_lanes = (lane % TILES) * ROWS + lane // TILES
+    for i in range(STEPS):
+        steps_ref[i] = steps[i]
+
+    def one(r, carry):
+        for k in range(FINISHED):
+            t = r * FINISHED + k
+            for i, value in enumerate(ambient_cell()):
+                moved = jnp.take_along_axis(fields[i, t], from_lanes, axis=1)
+                out_ref[i, pl.ds(t, ROWS, stride=TILES), :] = jnp.where(outside, jnp.float32(value), moved)
         return carry
 
-    lax.fori_loop(0, TILES, finish, 0)
+    lax.fori_loop(0, TILES // FINISHED, one, 0)
 
 
 def solution(mesh):
@@ -534,10 +611,11 @@
         f32 = jnp.float32
         tile = (TILES, ROWS, LANES)
         dma = pltpu.SemaphoreType.DMA
-        return pl.pallas_call(
+        labels, jitter = (pltpu.with_memory_space_constraint(a, pltpu.HBM) for a in (labels, jitter))
+        fields, steps = pl.pallas_call(
             functools.partial(kernel, sizes),
-            out_shape=(jax.ShapeDtypeStruct((6, *block), f32), jax.ShapeDtypeStruct((STEPS,), f32)),
-            in_specs=[pl.BlockSpec(memory_space=pl.ANY)] * 2,
+            out_shape=(jax.ShapeDtypeStruct((6, *tile), f32), jax.ShapeDtypeStruct((STEPS,), f32)),
+            in_specs=[pl.BlockSpec(memory_space=pltpu.HBM)] * 2,
             out_specs=(pl.BlockSpec(memory_space=pltpu.VMEM), pl.BlockSpec(memory_space=pltpu.SMEM)),
             scratch_shapes=[
                 pltpu.VMEM(block, jnp.int32),
@@ -547,12 +625,13 @@
                 pltpu.VMEM((6, TILES + 2 * GHOST, ROWS, LANES), f32),
                 pltpu.VMEM((6, TILES + 2 * GHOST, ROWS, LANES), f32),
                 pltpu.VMEM((6, *tile), f32),
-                pltpu.VMEM((6, *tile), f32),
                 pltpu.VMEM((2, 6, TILES + 3, ROWS, LANES), f32),
                 pltpu.VMEM((2, 6, TILES + 3, ROWS, LANES), f32),
                 pltpu.VMEM((6, TILES + 2, ROWS, LANES), f32),
                 pltpu.VMEM((6, TILES + 2, ROWS, LANES), f32),
                 pltpu.VMEM((6, *tile), f32),
+                pltpu.VMEM((6, 2, 24, LANES), f32),
+                pltpu.VMEM((6, 2, ROWS, LANES), f32),
                 pltpu.VMEM((ROWS, LANES), f32),
                 pltpu.VMEM((2, 18, 1, LANES), f32),
                 pltpu.VMEM((2, 18, 1, LANES), f32),
@@ -565,15 +644,24 @@
                 dma((2,)),
                 dma((2,)),
                 dma((2,)),
-                dma((STAGES, 4)),
-                dma((STAGES, 4)),
+                dma((2, 4)),
+                dma((2, 4)),
                 dma((STEPS, first)),
                 dma((STEPS, first)),
                 dma((STEPS, second)),
                 dma((STEPS, second)),
             ],
-            compiler_params=pltpu.CompilerParams(collective_id=0, has_side_effects=True),
+            compiler_params=pltpu.CompilerParams(
+                collective_id=0, has_side_effects=True, vmem_limit_bytes=VMEM_BYTES
+            ),
         )(labels, jitter)
+        return pl.pallas_call(
+            functools.partial(finish, ax_size),
+            out_shape=(jax.ShapeDtypeStruct((6, *block), f32), jax.ShapeDtypeStruct((STEPS,), f32)),
+            in_specs=[pl.BlockSpec(memory_space=pltpu.VMEM), pl.BlockSpec(memory_space=pltpu.SMEM)],
+            out_specs=(pl.BlockSpec(memory_space=pltpu.VMEM), pl.BlockSpec(memory_space=pltpu.SMEM)),
+            compiler_params=pltpu.CompilerParams(vmem_limit_bytes=VMEM_BYTES),
+        )(fields, steps)
 
     return jax.shard_map(
         shards, mesh=mesh, in_specs=(P("ax", "rad"),) * 2, out_specs=(P(None, "ax", "rad"), P()), check_vma=False

time: 87.8 us -> 70.2 us (0.80)
  Pallas kernels: 84.7 us -> 69.5 us
  local copies, waits for them, and re-layouts: 2.28 us -> 0 us
    pallas_call x1, Pallas kernels: 84.7 us -> 67.7 us  [shards(): pl.pallas_call(functools.partial(kernel, sizes), out_shape=(jax.ShapeDtyp...]
    unnamed x4 -> x0, local copies, waits for them, and re-layouts: 2.28 us -> none
    pallas_call x0 -> x1, Pallas kernels: none -> 1.79 us  [shards(): pl.pallas_call(functools.partial(finish, ax_size), out_shape=(jax.ShapeDt...]
where the time goes in v3:
time: 70.2 us; the launch traced here: 70.1 us
  Pallas kernels  69.5 us (99%)
    pallas_call x1, Pallas kernels, shards(): pl.pallas_call(functools.partial(kernel, sizes), out_shape=(jax.ShapeDtyp...  67.7 us
    pallas_call x1, Pallas kernels, shards(): pl.pallas_call(functools.partial(finish, ax_size), out_shape=(jax.ShapeDt...  1.79 us

profile of v3, /device:TPU:1, one launch (start us, length us, event | category | flops | bytes accessed | tf_op | source)
XLA Modules:
  0.0 70.1 jit_solution(1138532667622465026)
XLA Ops:
  0.6 67.7 %shard_map.41 = (f32[6,16,8,128]{3,2,1,0:T(8,128)S(1)}, f32[3]{0:T(128)S(1)}) custom-call(s32[128,128]{1,0:T(8,128)} %labels_hbm.1, f32[128,128]{1,0:T(8,128)} %jitter_hbm.1), custom_call_target="tpu_custom_call" | custom-call | tf_op jit(solution)/shard_map/pallas_call | solution.py:615
  68.3 1.8 %shard_map.42 = (f32[6,128,128]{2,1,0:T(8,128)}, f32[3]{0:T(128)}) custom-call(f32[6,16,8,128]{3,2,1,0:T(8,128)S(1)} %get-tuple-element.4.fields, f32[3]{0:T(128)S(1)} %get-tuple-element.5.steps), custom_call_target="tpu_custom_call" | custom-call | tf_op jit(solution)/shard_map/pallas_call | solution.py:658

commit v4 on v3

--- a/solution.py
+++ b/solution.py
@@ -173,6 +173,10 @@
     return [q_one * scaled, q_two * scaled, *moments, (energy + p) * speed, fraction, star]
 
 
+def far_first(size):
+    return sorted(range(size), key=lambda d: -min(d, size - d))
+
+
 def kernel(
     sizes,
     labels_hbm,
@@ -191,6 +195,7 @@
     axial_rate,
     radial_rate,
     turned,
+    total,
     strip,
     strip_rate,
     dt_ref,
@@ -224,14 +229,14 @@
 
     first_group = [
         at(lax.rem(z + dz, z_size), x, lax.rem(core + dc, core_size), rad)
-        for dz in range(z_size)
+        for dz in far_first(z_size)
         for dc in range(core_size)
         if (dz, dc) != (0, 0)
     ]
     second_group = [
         at(z, lax.rem(x + dx, x_size), core, lax.rem(rad + dr, rad_size))
-        for dx in range(x_size)
-        for dr in range(rad_size)
+        for dx in far_first(x_size)
+        for dr in far_first(rad_size)
         if (dx, dr) != (0, 0)
     ]
     ax_next = (lax.rem(ax + 1, ax_size), rad)
@@ -265,8 +270,8 @@
             pltpu.make_async_remote_copy(
                 src_ref=max_first.at[step],
                 dst_ref=got_first.at[step, i],
-                send_sem=first_send.at[step, i],
-                recv_sem=first_recv.at[step, i],
+                send_sem=first_send.at[step],
+                recv_sem=first_recv.at[step],
                 device_id=device,
                 device_id_type=MESH,
             )
@@ -278,13 +283,26 @@
             pltpu.make_async_remote_copy(
                 src_ref=max_second.at[step],
                 dst_ref=got_second.at[step, i],
-                send_sem=second_send.at[step, i],
-                recv_sem=second_recv.at[step, i],
+                send_sem=second_send.at[step],
+                recv_sem=second_recv.at[step],
                 device_id=device,
                 device_id_type=MESH,
             )
             for i, device in enumerate(second_group)
         ]
+
+    def whole_phase(step, second):
+        got, send, recv, group = (
+            (got_second, second_send, second_recv, second_group) if second else (got_first, first_send, first_recv, first_group)
+        )
+        return pltpu.make_async_remote_copy(
+            src_ref=got.at[step],
+            dst_ref=got.at[step],
+            send_sem=send.at[step],
+            recv_sem=recv.at[step],
+            device_id=group[0],
+            device_id_type=MESH,
+        )
 
     def halo_copies(stage, which=(0, 1, 2, 3)):
         parity = lax.rem(stage, 2)
@@ -337,8 +355,7 @@
         copy.wait()
 
     def second_phase(step):
-        for copy in first_copies(step):
-            copy.wait_recv()
+        whole_phase(step, False).wait_recv()
         max_second[step] = jnp.maximum(max_first[step], jnp.max(got_first[step], axis=0))
         for copy in second_copies(step):
             copy.start()
@@ -443,25 +460,58 @@
 
         lax.fori_loop(0, (TILES + 2) // FACES, some, (jnp.zeros((ROWS, LANES), jnp.float32),) * 7)
 
-    def send_axial_rims(stage):
-        take_rims(axial_cells, send_axial)
+    def send_axial_rims(stage, cells=axial_cells):
+        take_rims(cells, send_axial)
         for copy in halo_copies(stage, (0, 1)):
             copy.start()
 
-    def send_radial_rims(stage):
+    def turn_cells(axial, radial):
         def turn(r, carry):
             for k in range(TURNS):
                 i = r * TURNS + k
-                block = axial_cells[i, GHOST : GHOST + TILES].reshape(LANES, LANES)
-                radial_cells[i, GHOST : GHOST + TILES] = block.T.reshape(TILES, ROWS, LANES)
+                block = axial[i, GHOST : GHOST + TILES].reshape(LANES, LANES)
+                radial[i, GHOST : GHOST + TILES] = block.T.reshape(TILES, ROWS, LANES)
             return carry
 
         lax.fori_loop(0, 6 // TURNS, turn, 0)
-        take_rims(radial_cells, send_radial)
+
+    def send_radial_rims(stage, cells=radial_cells):
+        take_rims(cells, send_radial)
         for copy in halo_copies(stage, (2, 3)):
             copy.start()
 
+    def whole_rate(t, q_one, q_two, u, v, p, a, energy):
+        over = v * per_radius
+        carried = (q_one + q_two) * over
+        source = (q_one * over, q_two * over, u * carried, v * carried, (energy + p) * over)
+        change = [axial_rate[i, t + 1] + turned[i, t] for i in range(6)]
+        return [change[i] - source[i] for i in range(5)] + [change[5]]
+
+    def primitives(fields):
+        density = fields[0] + fields[1]
+        gamma_sum, stiff_sum = mixture(fields[5])
+        inverse = 1.0 / (density * gamma_sum)
+        per_density = inverse * gamma_sum
+        u = fields[2] * per_density
+        v = fields[3] * per_density
+        p = (fields[4] - 0.5 * (fields[2] * u + fields[3] * v) - stiff_sum) * (inverse * density)
+        return fields[0], fields[1], u, v, p, fields[5]
+
+    def advance_rims(recv, stage):
+        dt = dt_ref[0:1, :]
+        for side in range(2):
+            old = [recv[stage - 1, side, 3 * i : 3 * i + 3] for i in range(6)]
+            change = [recv[stage, side, 3 * i : 3 * i + 3] for i in range(6)]
+            q_one, q_two, u, v, p, a = old
+            density = q_one + q_two
+            gamma_sum, stiff_sum = mixture(a)
+            energy = gamma_sum * p + stiff_sum + 0.5 * density * (u * u + v * v)
+            before = (q_one, q_two, density * u, density * v, energy, a)
+            for i, value in enumerate(primitives([b + dt * c for b, c in zip(before, change)])):
+                recv[stage, side, 3 * i : 3 * i + 3] = value
+
     send_axial_rims(0)
+    turn_cells(axial_cells, radial_cells)
     send_radial_rims(0)
 
     def stage_body(stage, carry):
@@ -479,6 +529,12 @@
 
         for copy in halos:
             copy.wait_recv()
+
+        @pl.when(section == 1)
+        def _():
+            advance_rims(recv_axial, stage)
+            advance_rims(recv_radial, stage)
+
         rim_strip(recv_axial, stage, 0, block_first, block_last)
         rim_strip(recv_radial, stage, 1, wall, outer)
         strip_rates()
@@ -496,22 +552,27 @@
 
         lax.fori_loop(0, 6 // TURNS, turn_back, 0)
 
+        for copy in halos:
+            copy.wait_send()
+
         @pl.when(section == 0)
         def _():
-            sends = second_copies(step)
-            for copy in sends:
-                copy.wait_recv()
+            def rates(t, carry):
+                for i, value in enumerate(whole_rate(t, *(axial_cells[i, GHOST + t] for i in range(6)), fields[4, t])):
+                    total[0, i, GHOST + t] = value
+                return carry
+
+            lax.fori_loop(0, TILES, rates, 0)
+            send_axial_rims(stage + 1, total.at[0])
+            turn_cells(total.at[0], total.at[1])
+            send_radial_rims(stage + 1, total.at[1])
+            whole_phase(step, True).wait_recv()
             top = jnp.maximum(max_second[step], jnp.max(got_second[step], axis=0))
             dt = CFL_NUMBER / jnp.broadcast_to(jnp.max(top, axis=1, keepdims=True), (ROWS, LANES))
             dt_ref[...] = dt
             steps_ref[step] = jnp.max(dt)
-            for copy in sends:
-                copy.wait_send()
-            for copy in first_copies(step):
-                copy.wait_send()
-
-        for copy in halos:
-            copy.wait_send()
+            whole_phase(step, True).wait_send()
+            whole_phase(step, False).wait_send()
 
         third = jnp.float32(1.0 / 3.0)
         keep = jnp.where(section == 0, 0.0, jnp.where(section == 1, 0.75, third))
@@ -521,30 +582,20 @@
 
         def update(tiles, most):
             for t in tiles:
-                q_one, q_two, u, v, p, a = (axial_cells[i, GHOST + t] for i in range(6))
                 old = [fields[i, t] for i in range(6)]
-                over = v * per_radius
-                carried = (q_one + q_two) * over
-                source = (q_one * over, q_two * over, u * carried, v * carried, (old[4] + p) * over)
+                change = whole_rate(t, *(axial_cells[i, GHOST + t] for i in range(6)), old[4])
                 new = []
                 for i in range(6):
-                    change = axial_rate[i, t + 1] + turned[i, t]
-                    if i < 5:
-                        change = change - source[i]
                     start = base[i, t]
-                    value = keep * start + take * (old[i] + dt * change)
+                    value = keep * start + take * (old[i] + dt * change[i])
                     fields[i, t] = value
                     base[i, t] = jnp.where(closing, value, start)
                     new.append(value)
-                density = new[0] + new[1]
-                gamma_sum, stiff_sum = mixture(new[5])
-                inverse = 1.0 / (density * gamma_sum)
-                per_density = inverse * gamma_sum
-                u = new[2] * per_density
-                v = new[3] * per_density
-                p = (new[4] - 0.5 * (new[2] * u + new[3] * v) - stiff_sum) * (inverse * density)
-                for i, value in enumerate((new[0], new[1], u, v, p, new[5])):
+                q_one, q_two, u, v, p, a = primitives(new)
+                for i, value in enumerate((q_one, q_two, u, v, p, a)):
                     axial_cells[i, GHOST + t] = value
+                density = q_one + q_two
+                gamma_sum, stiff_sum = mixture(a)
                 speed = jnp.abs(u) + jnp.abs(v) + celerity_of(density, p, gamma_sum, stiff_sum)
                 most = jnp.maximum(most, speed)
             return most
@@ -556,7 +607,7 @@
             jnp.zeros((ROWS, LANES), jnp.float32),
         )
 
-        @pl.when(stage < STAGES - 1)
+        @pl.when(jnp.logical_and(section > 0, stage < STAGES - 1))
         def _():
             send_axial_rims(stage + 1)
 
@@ -574,6 +625,10 @@
                 copy.start()
 
         @pl.when(stage < STAGES - 1)
+        def _():
+            turn_cells(axial_cells, radial_cells)
+
+        @pl.when(jnp.logical_and(section > 0, stage < STAGES - 1))
         def _():
             send_radial_rims(stage + 1)
 
@@ -630,6 +685,7 @@
                 pltpu.VMEM((6, TILES + 2, ROWS, LANES), f32),
                 pltpu.VMEM((6, TILES + 2, ROWS, LANES), f32),
                 pltpu.VMEM((6, *tile), f32),
+                pltpu.VMEM((2, 6, TILES + 2 * GHOST, ROWS, LANES), f32),
                 pltpu.VMEM((6, 2, 24, LANES), f32),
                 pltpu.VMEM((6, 2, ROWS, LANES), f32),
                 pltpu.VMEM((ROWS, LANES), f32),
@@ -646,10 +702,10 @@
                 dma((2,)),
                 dma((2, 4)),
                 dma((2, 4)),
-                dma((STEPS, first)),
-                dma((STEPS, first)),
-                dma((STEPS, second)),
-                dma((STEPS, second)),
+                dma((STEPS,)),
+                dma((STEPS,)),
+                dma((STEPS,)),
+                dma((STEPS,)),
             ],
             compiler_params=pltpu.CompilerParams(
                 collective_id=0, has_side_effects=True, vmem_limit_bytes=VMEM_BYTES

time: 70.2 us -> 65.9 us (0.939)
  Pallas kernels: 69.5 us -> 65.1 us
    pallas_call x1, Pallas kernels: 67.7 us -> 63.3 us  [shards(): pl.pallas_call(functools.partial(kernel, sizes), out_shape=(jax.ShapeDtyp...]
where the time goes in v4:
time: 65.9 us; the launch traced here: 65.7 us
  Pallas kernels  65.1 us (99%)
    pallas_call x1, Pallas kernels, shards(): pl.pallas_call(functools.partial(kernel, sizes), out_shape=(jax.ShapeDtyp...  63.3 us
    pallas_call x1, Pallas kernels, shards(): pl.pallas_call(functools.partial(finish, ax_size), out_shape=(jax.ShapeDt...  1.79 us

profile of v4, /device:TPU:1, one launch (start us, length us, event | category | flops | bytes accessed | tf_op | source)
XLA Modules:
  0.0 65.7 jit_solution(7554310016850761397)
XLA Ops:
  0.6 63.3 %shard_map.41 = (f32[6,16,8,128]{3,2,1,0:T(8,128)S(1)}, f32[3]{0:T(128)S(1)}) custom-call(s32[128,128]{1,0:T(8,128)} %labels_hbm.1, f32[128,128]{1,0:T(8,128)} %jitter_hbm.1), custom_call_target="tpu_custom_call" | custom-call | tf_op jit(solution)/shard_map/pallas_call | solution.py:670
  64.0 1.8 %shard_map.42 = (f32[6,128,128]{2,1,0:T(8,128)}, f32[3]{0:T(128)}) custom-call(f32[6,16,8,128]{3,2,1,0:T(8,128)S(1)} %get-tuple-element.4.fields, f32[3]{0:T(128)S(1)} %get-tuple-element.5.steps), custom_call_target="tpu_custom_call" | custom-call | tf_op jit(solution)/shard_map/pallas_call | solution.py:714

commit v5 on v4

--- a/solution.py
+++ b/solution.py
@@ -79,10 +79,10 @@
     return top * lax.rsqrt(top * (gamma_sum * density))
 
 
-def weno_terms(ea, eb, ec, ed, da, db, dc, ta, tb, tc, ga, gb):
-    smooth_zero = ta + eb * (eb + da)
-    smooth_one = tb + eb * ec
-    smooth_two = tc + ec * (ec - dc)
+def weno_terms(ha, hb, da, db, dc, ta, tb, tc, ga, gb):
+    smooth_zero = ta + ha * (ha + da)
+    smooth_one = tb + ha * hb
+    smooth_two = tc + hb * (hb - dc)
     square_zero = smooth_zero * smooth_zero
     square_one = smooth_one * smooth_one
     square_two = smooth_two * smooth_two
@@ -91,38 +91,36 @@
     weight_two = square_zero * square_one
     low = weight_zero * ga
     high = weight_two * gb
-    both = low + high
-    twice = both + both
     common = 6.0 * weight_one + (weight_zero + weight_two)
-    upper = (twice + high) / (common + (weight_two + weight_two))
-    lower = (twice + low) / (common + (weight_zero + weight_zero))
+    upper = (low + 1.5 * high) / (common + (weight_two + weight_two))
+    lower = (high + 1.5 * low) / (common + (weight_zero + weight_zero))
     return upper, lower
 
 
 def weno_cell(cells):
     m2, m1, c, p1, p2 = cells
-    ea, eb, ec, ed = m1 - m2, c - m1, p1 - c, p2 - p1
-    da, db, dc = eb - ea, ec - eb, ed - ec
-    ta, tb, tc = (d * (d * (4.0 / 3.0)) + WENO_EPS for d in (da, db, dc))
-    qa, qb, qc = (d * (1.0 / 6.0) for d in (da, db, dc))
-    upper, lower = weno_terms(ea, eb, ec, ed, da, db, dc, ta, tb, tc, qb - qa, qc - qb)
-    base = c + (qb + qb)
-    return base + 0.5 * eb - upper, base - 0.5 * ec + lower
+    h0, ha, hb, h3 = (0.5 * (y - x) for x, y in ((m2, m1), (m1, c), (c, p1), (p1, p2)))
+    da, db, dc = ha - h0, hb - ha, h3 - hb
+    ta, tb, tc = (d * (d * (4.0 / 3.0)) + 0.25 * WENO_EPS for d in (da, db, dc))
+    qa, qb, qc = (d * (2.0 / 3.0) for d in (da, db, dc))
+    upper, lower = weno_terms(ha, hb, da, db, dc, ta, tb, tc, qb - qa, qc - qb)
+    base = c + qb
+    return base + ha - upper, base - hb + lower
 
 
 def weno_run(w, count):
-    e = w[1:] - w[:-1]
-    d = e[1:] - e[:-1]
-    t = d * (d * (4.0 / 3.0)) + WENO_EPS
-    q = d * (1.0 / 6.0)
+    h = 0.5 * (w[1:] - w[:-1])
+    d = h[1:] - h[:-1]
+    t = d * (d * (4.0 / 3.0)) + 0.25 * WENO_EPS
+    q = d * (2.0 / 3.0)
     g = q[1:] - q[:-1]
     n = count
+    ha, hb = h[1 : n + 1], h[2 : n + 2]
     upper, lower = weno_terms(
-        e[:n], e[1 : n + 1], e[2 : n + 2], e[3:], d[:n], d[1 : n + 1], d[2:], t[:n], t[1 : n + 1], t[2:], g[:n], g[1:]
+        ha, hb, d[:n], d[1 : n + 1], d[2:], t[:n], t[1 : n + 1], t[2:], g[:n], g[1:]
     )
-    middle = q[1 : n + 1]
-    base = w[2 : n + 2] + (middle + middle)
-    return base + 0.5 * e[1 : n + 1] - upper, base - 0.5 * e[2 : n + 2] + lower
+    base = w[2 : n + 2] + q[1 : n + 1]
+    return base + ha - upper, base - hb + lower
 
 
 def hllc(left, right, normal):
@@ -438,19 +436,37 @@
                 radial_rate[i, 1 + k, 0:1, :] = strip_rate[q, 1, 2 * k : 2 * k + 1, :]
                 radial_rate[i, TILES - 2 + k, ROWS - 1 : ROWS, :] = strip_rate[q, 1, 2 * k + 1 : 2 * k + 2, :]
 
-    def all_states(i, carry):
-        for which, cells in enumerate((axial_cells, radial_cells)):
-            for first in range(0, TILES + 2, RUN):
-                up, down = weno_run(cells[i, first : first + RUN + 4], RUN)
-                upper[which, i, first : first + RUN] = up
-                lower[which, i, first : first + RUN] = down
-        return carry
-
-    def faces(cells, which, rate, normal):
+    def rim_ghosts(cells, recv, stage, which, at_low, at_high):
+        for i in range(6):
+            high = cells[i, GHOST + TILES - 1, ROWS - 1 : ROWS, :]
+            for k in range(GHOST):
+                if which:
+                    low = cells[i, 2 * GHOST - 1 - k, 0:1, :]
+                    if i == 3:
+                        low = -low
+                else:
+                    low = cells[i, GHOST, 0:1, :]
+                cells[i, k, 0:1, :] = jnp.where(at_low, low, recv[stage, 0, 3 * i + k])
+                cells[i, GHOST + TILES + k, ROWS - 1 : ROWS, :] = jnp.where(at_high, high, recv[stage, 1, 3 * i + k])
+
+    def states(cells, which, runs):
+        def one(i, carry):
+            for first, count in runs:
+                up, down = weno_run(cells[i, first : first + count + 4], count)
+                upper[which, i, first : first + count] = up
+                lower[which, i, first : first + count] = down
+            return carry
+
+        lax.fori_loop(0, 6, one, 0)
+
+    def face(which, f, normal):
+        return hllc([upper[which, i, f] for i in range(6)], [lower[which, i, f + 1] for i in range(6)], normal)
+
+    def faces(cells, which, rate, normal, first, below, rounds, count, stride):
         def some(r, below):
-            for k in range(FACES):
-                f = r * FACES + k
-                above = hllc([upper[which, i, f] for i in range(6)], [lower[which, i, f + 1] for i in range(6)], normal)
+            for k in range(count):
+                f = first + r * stride + k
+                above = face(which, f, normal)
                 change = [b - a for b, a in zip(below, above)]
                 change[5] = change[5] - cells[5, f + 2] * change[6]
                 for i in range(6):
@@ -458,7 +474,21 @@
                 below = tuple(above)
             return below
 
-        lax.fori_loop(0, (TILES + 2) // FACES, some, (jnp.zeros((ROWS, LANES), jnp.float32),) * 7)
+        lax.fori_loop(0, rounds, some, below)
+
+    still = (jnp.zeros((ROWS, LANES), jnp.float32),) * 7
+
+    def radial_sweep():
+        states(radial_cells, 1, [(first, RUN) for first in range(0, TILES + 2, RUN)])
+        faces(radial_cells, 1, radial_rate, 3, 0, still, (TILES + 2) // FACES, FACES, FACES)
+
+    def axial_ends():
+        states(axial_cells, 0, [(0, 6), (12, 6)])
+        faces(axial_cells, 0, axial_rate, 2, 0, still, 2, 4, 13)
+
+    def axial_middle():
+        states(axial_cells, 0, [(6, 6)])
+        faces(axial_cells, 0, axial_rate, 2, 4, tuple(face(0, 3, 2)), 2, 5, 5)
 
     def send_axial_rims(stage, cells=axial_cells):
         take_rims(cells, send_axial)
@@ -510,6 +540,7 @@
             for i, value in enumerate(primitives([b + dt * c for b, c in zip(before, change)])):
                 recv[stage, side, 3 * i : 3 * i + 3] = value
 
+    dt_ref[...] = jnp.zeros_like(dt_ref)
     send_axial_rims(0)
     turn_cells(axial_cells, radial_cells)
     send_radial_rims(0)
@@ -521,23 +552,38 @@
 
         wrapped(axial_cells)
         wrapped(radial_cells)
-        own_strip(axial_cells, 0)
-        own_strip(radial_cells, 1)
-        lax.fori_loop(0, 6, all_states, 0)
-        faces(axial_cells, 0, axial_rate, 2)
-        faces(radial_cells, 1, radial_rate, 3)
-
-        for copy in halos:
-            copy.wait_recv()
-
-        @pl.when(section == 1)
-        def _():
+
+        early = jnp.logical_and(section == 1, step > 0)
+
+        @pl.when(early)
+        def _():
+            for copy in halos:
+                copy.wait_recv()
             advance_rims(recv_axial, stage)
             advance_rims(recv_radial, stage)
-
-        rim_strip(recv_axial, stage, 0, block_first, block_last)
-        rim_strip(recv_radial, stage, 1, wall, outer)
-        strip_rates()
+            rim_ghosts(axial_cells, recv_axial, stage, 0, block_first, block_last)
+            rim_ghosts(radial_cells, recv_radial, stage, 1, wall, outer)
+
+        radial_sweep()
+        axial_ends()
+
+        @pl.when(jnp.logical_not(early))
+        def _():
+            axial_middle()
+            steps_ref[step] = jnp.max(dt_ref[...])
+            own_strip(axial_cells, 0)
+            own_strip(radial_cells, 1)
+            for copy in halo_copies(stage):
+                copy.wait_recv()
+
+            @pl.when(section == 1)
+            def _():
+                advance_rims(recv_axial, stage)
+                advance_rims(recv_radial, stage)
+
+            rim_strip(recv_axial, stage, 0, block_first, block_last)
+            rim_strip(recv_radial, stage, 1, wall, outer)
+            strip_rates()
 
         @pl.when(jnp.logical_and(section == 0, step > 0))
         def _():
@@ -570,7 +616,6 @@
             top = jnp.maximum(max_second[step], jnp.max(got_second[step], axis=0))
             dt = CFL_NUMBER / jnp.broadcast_to(jnp.max(top, axis=1, keepdims=True), (ROWS, LANES))
             dt_ref[...] = dt
-            steps_ref[step] = jnp.max(dt)
             whole_phase(step, True).wait_send()
             whole_phase(step, False).wait_send()
 
@@ -610,6 +655,10 @@
         @pl.when(jnp.logical_and(section > 0, stage < STAGES - 1))
         def _():
             send_axial_rims(stage + 1)
+
+        @pl.when(early)
+        def _():
+            axial_middle()
 
         most = lax.fori_loop(
             0,

time: 65.9 us -> 65.5 us (level)
  no operation moved by 1% of the time
where the time goes in v5:
time: 65.5 us; the launch traced here: 65.3 us
  Pallas kernels  64.7 us (99%)
    pallas_call x1, Pallas kernels, shards(): pl.pallas_call(functools.partial(kernel, sizes), out_shape=(jax.ShapeDtyp...  62.9 us
    pallas_call x1, Pallas kernels, shards(): pl.pallas_call(functools.partial(finish, ax_size), out_shape=(jax.ShapeDt...  1.79 us

profile of v5, /device:TPU:1, one launch (start us, length us, event | category | flops | bytes accessed | tf_op | source)
XLA Modules:
  0.0 65.3 jit_solution(7920419988944625910)
XLA Ops:
  0.6 62.9 %shard_map.41 = (f32[6,16,8,128]{3,2,1,0:T(8,128)S(1)}, f32[3]{0:T(128)S(1)}) custom-call(s32[128,128]{1,0:T(8,128)} %labels_hbm.1, f32[128,128]{1,0:T(8,128)} %jitter_hbm.1), custom_call_target="tpu_custom_call" | custom-call | tf_op jit(solution)/shard_map/pallas_call | solution.py:719
  63.5 1.8 %shard_map.42 = (f32[6,128,128]{2,1,0:T(8,128)}, f32[3]{0:T(128)}) custom-call(f32[6,16,8,128]{3,2,1,0:T(8,128)S(1)} %get-tuple-element.4.fields, f32[3]{0:T(128)S(1)} %get-tuple-element.5.steps), custom_call_target="tpu_custom_call" | custom-call | tf_op jit(solution)/shard_map/pallas_call | solution.py:763

commit v6 on v5

--- a/solution.py
+++ b/solution.py
@@ -254,12 +254,13 @@
         pltpu.make_async_copy(labels_hbm, own_labels, local_sem.at[0]),
         pltpu.make_async_copy(jitter_hbm, own_jitter, local_sem.at[1]),
     ]
-    for copy in copies:
-        copy.start()
     barrier = pltpu.get_barrier_semaphore()
-    greeted = first_group + second_group + [ax_next, ax_last]
+    greeted = second_group[:8] + first_group[:8] + second_group[8:] + first_group[8:] + [ax_next, ax_last]
     for device in greeted:
         pl.semaphore_signal(barrier, inc=1, device_id=device, device_id_type=MESH)
+        if device is greeted[0]:
+            for copy in copies:
+                copy.start()
     for copy in copies:
         copy.wait()
 
@@ -616,8 +617,6 @@
             top = jnp.maximum(max_second[step], jnp.max(got_second[step], axis=0))
             dt = CFL_NUMBER / jnp.broadcast_to(jnp.max(top, axis=1, keepdims=True), (ROWS, LANES))
             dt_ref[...] = dt
-            whole_phase(step, True).wait_send()
-            whole_phase(step, False).wait_send()
 
         third = jnp.float32(1.0 / 3.0)
         keep = jnp.where(section == 0, 0.0, jnp.where(section == 1, 0.75, third))
@@ -666,6 +665,11 @@
             lambda r, m: update([GHOST + r * UPDATES + k for k in range(UPDATES)], m),
             most,
         )
+
+        @pl.when(section == 1)
+        def _():
+            whole_phase(step, True).wait_send()
+            whole_phase(step, False).wait_send()
 
         @pl.when(jnp.logical_and(closing, step < STEPS - 1))
         def _():

time: 65.5 us -> 65.4 us (level)
  no operation moved by 1% of the time
where the time goes in v6:
time: 65.4 us; the launch traced here: 65.2 us
  Pallas kernels  64.6 us (99%)
    pallas_call x1, Pallas kernels, shards(): pl.pallas_call(functools.partial(kernel, sizes), out_shape=(jax.ShapeDtyp...  62.8 us
    pallas_call x1, Pallas kernels, shards(): pl.pallas_call(functools.partial(finish, ax_size), out_shape=(jax.ShapeDt...  1.79 us

profile of v6, /device:TPU:1, one launch (start us, length us, event | category | flops | bytes accessed | tf_op | source)
XLA Modules:
  0.0 65.2 jit_solution(656541342482560074)
XLA Ops:
  0.6 62.8 %shard_map.41 = (f32[6,16,8,128]{3,2,1,0:T(8,128)S(1)}, f32[3]{0:T(128)S(1)}) custom-call(s32[128,128]{1,0:T(8,128)} %labels_hbm.1, f32[128,128]{1,0:T(8,128)} %jitter_hbm.1), custom_call_target="tpu_custom_call" | custom-call | tf_op jit(solution)/shard_map/pallas_call | solution.py:723
  63.5 1.8 %shard_map.42 = (f32[6,128,128]{2,1,0:T(8,128)}, f32[3]{0:T(128)}) custom-call(f32[6,16,8,128]{3,2,1,0:T(8,128)S(1)} %get-tuple-element.4.fields, f32[3]{0:T(128)S(1)} %get-tuple-element.5.steps), custom_call_target="tpu_custom_call" | custom-call | tf_op jit(solution)/shard_map/pallas_call | solution.py:767
